TPU v7x, 32 devices: a whole 2x2x4 slice. The times are simulated.
32 devices in a mesh: gx: 4 (over x, core), gy: 8 (over z, y).
Axes of the slice: x: 2, y: 2, z: 4, core: 2. Of those that a mesh axis runs over, the one named last changes fastest.
Arguments:
- queries: bfloat16 [4, 8, 128, 768], P('gx', 'gy'), may hold values from -40 to 40
- keys_values: bfloat16 [4, 8, 2, 128, 768], P('gx', 'gy'), may hold values from -10 to 10
- out_grad: bfloat16 [4, 8, 128, 768], P('gx', 'gy'), may hold values from -6 to 6
- pattern: int32 [4, 8, 9], P('gx', 'gy'), may hold values 0 or 1
Outputs:
- attended: bfloat16 [4, 8, 128, 768], P('gx', 'gy')
- query_grad: bfloat16 [4, 8, 128, 768], P('gx', 'gy')
- key_value_grad: bfloat16 [4, 8, 2, 128, 768], P('gx', 'gy')
All inputs are finite; a program needn't handle non-finite values. No bound on the sum of `pattern` on one device may be relied on, other than what follows from the above.
Results may differ from a plain program's by a relative error of at most 0.02.
Values may be sent and summed in bfloat16 or wider, within the bound.
No kernel may reach another device: no remote copies, remote signals or barrier semaphores. Data moves between devices by JAX's collectives and lax.ppermute only.
A program may use at most 128 MiB of HBM per device.

v0:
```python
import functools
import math

import jax
import jax.numpy as jnp
from jax import lax
from jax.experimental import pallas as pl
from jax.experimental.pallas import tpu as pltpu
from jax.sharding import PartitionSpec as P

E = 64
LANES = 128
PENALTY = 1e30
FOLD = math.log2(math.e) * float(E) ** (-0.5)
SCALE = float(E) ** (-0.5)
CONTRACT_LAST = (((1,), (1,)), ((), ()))


def pair_swap(value, axis, offset):
    pairs = []
    for first in range(offset, lax.axis_size(axis) - 1, 2):
        pairs += [(first, first + 1), (first + 1, first)]
    return lax.ppermute(value, axis, pairs)


def partner_swap(value, level):
    return lax.ppermute(value, "gx", [(i, i ^ (1 << level)) for i in range(lax.axis_size("gx"))])


def split_heads(block):
    low = lax.broadcasted_iota(jnp.int32, block.shape, 1) < E
    zero = jnp.zeros_like(block)
    return jnp.concatenate([jnp.where(low, block, zero), jnp.where(low, zero, block)], axis=0)


def join_heads(stacked):
    rows = stacked.shape[0] // 2
    low = lax.broadcasted_iota(jnp.int32, (rows, LANES), 1) < E
    return jnp.where(low, stacked[:rows], stacked[rows:])


def query_kernel(count, bias_ref, q_ref, do_ref, flags_ref, *refs):
    kv_refs = refs[:count]
    att_ref, dq_ref, stats_ref = refs[count:]
    rows, width = q_ref.shape
    heads = width // E
    lane = lax.broadcasted_iota(jnp.int32, (rows, LANES), 1)
    low = lane < E
    stats = jnp.zeros((rows, LANES), jnp.float32)
    for pair in range(width // LANES):
        cols = slice(pair * LANES, (pair + 1) * LANES)
        grad = do_ref[:, cols]
        keys = jnp.concatenate([r[0, :, cols] for r in kv_refs], axis=0)
        values = jnp.concatenate([r[1, :, cols] for r in kv_refs], axis=0)
        scores = lax.dot_general(
            split_heads(q_ref[:, cols]), keys, CONTRACT_LAST, preferred_element_type=jnp.float32
        )
        scores = jnp.concatenate(
            [scores[:, b * rows : (b + 1) * rows] + bias_ref[b] for b in range(count)], axis=1
        )
        largest = jnp.max(scores, axis=1, keepdims=True) * FOLD
        raised = jnp.exp2(scores * FOLD - largest)
        totals = jnp.sum(raised, axis=1, keepdims=True)
        inverse = 1.0 / totals
        attended = jnp.dot(
            raised.astype(jnp.bfloat16), values, preferred_element_type=jnp.float32
        )
        attended = join_heads(attended * inverse).astype(jnp.bfloat16)
        att_ref[:, cols] = attended
        product = grad.astype(jnp.float32) * attended.astype(jnp.float32)
        delta = jnp.concatenate(
            [
                jnp.sum(jnp.where(low, product, 0.0), axis=1, keepdims=True),
                jnp.sum(jnp.where(low, 0.0, product), axis=1, keepdims=True),
            ],
            axis=0,
        )
        prob_grad = lax.dot_general(
            split_heads(grad), values, CONTRACT_LAST, preferred_element_type=jnp.float32
        )
        score_grad = (raised * (prob_grad - delta)).astype(jnp.bfloat16)
        query_grad = jnp.dot(score_grad, keys, preferred_element_type=jnp.float32)
        dq_ref[:, cols] = join_heads(query_grad * (inverse * SCALE)).astype(jnp.bfloat16)
        level = largest + jnp.log2(totals)
        for half in range(2):
            head = 2 * pair + half
            part = slice(half * rows, (half + 1) * rows)
            stats = jnp.where(lane == head, level[part], stats)
            stats = jnp.where(lane == heads + head, delta[part], stats)
    turned = stats.T
    stats_ref[: 2 * heads] = turned[: 2 * heads]
    stats_ref[2 * heads :] = flags_ref[...]


def key_kernel(count, slots, index_ref, choose_ref, kv_ref, q_ref, do_ref, *refs):
    qd_refs = refs[: count - 1]
    stat_refs = refs[count - 1 : count + 2]
    out_ref = refs[count + 2]
    rows, width = q_ref.shape
    heads = width // E
    levels, deltas = [], []
    for b in range(count):
        stat = stat_refs[slots[b]][index_ref[b]]
        flag = jnp.sum(
            stat[2 * heads : 2 * heads + 1] * choose_ref[b : b + 1], axis=1, keepdims=True
        )
        levels.append(stat[:heads] + jnp.where(flag > 0.5, 0.0, PENALTY))
        deltas.append(stat[heads : 2 * heads])
    levels = jnp.concatenate(levels, axis=1)
    deltas = jnp.concatenate(deltas, axis=1)

    def per_head(table, pair):
        shape = (rows, table.shape[1])
        return jnp.concatenate(
            [jnp.broadcast_to(table[2 * pair + h : 2 * pair + h + 1], shape) for h in range(2)],
            axis=0,
        )

    for pair in range(width // LANES):
        cols = slice(pair * LANES, (pair + 1) * LANES)
        queries = jnp.concatenate([q_ref[:, cols]] + [r[0, :, cols] for r in qd_refs], axis=0)
        grads = jnp.concatenate([do_ref[:, cols]] + [r[1, :, cols] for r in qd_refs], axis=0)
        scores = lax.dot_general(
            split_heads(kv_ref[0, :, cols]),
            queries,
            CONTRACT_LAST,
            preferred_element_type=jnp.float32,
        )
        weights = jnp.exp2(scores * FOLD - per_head(levels, pair))
        value_grad = jnp.dot(
            weights.astype(jnp.bfloat16), grads, preferred_element_type=jnp.float32
        )
        prob_grad = lax.dot_general(
            split_heads(kv_ref[1, :, cols]),
            grads,
            CONTRACT_LAST,
            preferred_element_type=jnp.float32,
        )
        score_grad = (weights * (prob_grad - per_head(deltas, pair))).astype(jnp.bfloat16)
        key_grad = jnp.dot(score_grad, queries, preferred_element_type=jnp.float32)
        out_ref[0, :, cols] = (join_heads(key_grad) * SCALE).astype(jnp.bfloat16)
        out_ref[1, :, cols] = join_heads(value_grad).astype(jnp.bfloat16)


VMEM = pl.BlockSpec(memory_space=pltpu.VMEM)
SMEM = pl.BlockSpec(memory_space=pltpu.SMEM)


def cost(rows, width, count):
    return pl.CostEstimate(
        flops=8 * rows * rows * width * count,
        bytes_accessed=4 * rows * width * (count + 3),
        transcendentals=rows * rows * (width // E) * count,
    )


def per_device(queries, keys_values, out_grad, pattern):
    own_q, own_kv, own_do = queries[0, 0], keys_values[0, 0], out_grad[0, 0]
    rows, width = own_q.shape
    heads = width // E
    columns, lines = lax.axis_size("gx"), lax.axis_size("gy")
    levels = columns.bit_length() - 2
    column, line = lax.axis_index("gx"), lax.axis_index("gy")
    side = 1 - 2 * (column % 2)
    turn = 1 - 2 * (line % 2)

    def exchange_row(value):
        pair = pair_swap(value, "gx", 0)
        partners = [partner_swap(value, level) for level in range(1, levels + 1)]
        if columns == 4:
            other = pair_swap(partners[0], "gx", 0)
        else:
            other = pair_swap(value, "gx", 1)
        return [pair, other] + partners

    def exchange_lines(value):
        return pair_swap(value, "gy", 1), pair_swap(value, "gy", 0)

    def spread(value):
        return [value, pair_swap(value, "gx", 0), pair_swap(value, "gx", 1)]

    far_kv, near_kv = exchange_lines(own_kv)
    row_kv = exchange_row(own_kv)
    own_qd = jnp.stack([own_q, own_do])
    far_qd, near_qd = exchange_lines(own_qd)
    row_qd = exchange_row(own_qd)
    kv_blocks = [own_kv] + row_kv + spread(far_kv) + spread(near_kv)

    shift_x = [0, side, -side] + [0] * levels + [0, side, -side] * 2
    shift_y = [0] * (3 + levels) + [-turn] * 3 + [turn] * 3
    count = len(kv_blocks)
    slots = [0] * (3 + levels) + [1] * 3 + [2] * 3
    shift_x = jnp.stack([jnp.asarray(v, jnp.int32) for v in shift_x])
    shift_y = jnp.stack([jnp.asarray(v, jnp.int32) for v in shift_y])
    position = jnp.arange(count)
    level = position - 2
    is_partner = (level >= 1) & (level <= levels)
    place = (shift_x + 1) * 3 + shift_y + 1
    flag = jnp.where(is_partner, 7 + level, jnp.where(place < 4, place, place - 1))
    mirrored = jnp.where(is_partner, 7 + level, 7 - flag)
    target_x = jnp.where(is_partner, column ^ (1 << jnp.maximum(level, 0)), column + shift_x)
    target_y = line + shift_y
    inside = (target_x >= 0) & (target_x < columns) & (target_y >= 0) & (target_y < lines)
    is_own = position == 0
    bits = pattern[0, 0]
    kinds = jnp.arange(bits.shape[0])
    chosen = jnp.sum(jnp.where(flag[:, None] == kinds[None], bits[None], 0), axis=1) > 0
    bias = jnp.where(is_own | (inside & chosen), 0.0, -PENALTY).astype(jnp.float32)
    index = jnp.clip(target_x, 0, columns - 1).astype(jnp.int32)
    lanes = jnp.arange(LANES)
    wanted = jnp.where(is_own, LANES - 1, jnp.where(inside, mirrored, -1))
    choose = (wanted[:, None] == lanes[None]).astype(jnp.float32)
    flags = jnp.pad((bits > 0).astype(jnp.float32), (0, LANES - bits.shape[0]))
    flags = jnp.where(lanes == LANES - 1, 1.0, flags)
    flags = jnp.broadcast_to(flags[None], (8, LANES))

    attended, query_grad, stats = pl.pallas_call(
        functools.partial(query_kernel, count),
        out_shape=(
            jax.ShapeDtypeStruct((rows, width), jnp.bfloat16),
            jax.ShapeDtypeStruct((rows, width), jnp.bfloat16),
            jax.ShapeDtypeStruct((2 * heads + 8, LANES), jnp.float32),
        ),
        in_specs=[SMEM] + [VMEM] * (3 + count),
        out_specs=(VMEM, VMEM, VMEM),
        cost_estimate=cost(rows, width, count),
    )(bias, own_q, own_do, flags, *kv_blocks)

    row_stats = lax.all_gather(stats, "gx")
    far_stats, near_stats = exchange_lines(row_stats)
    qd_blocks = row_qd + spread(far_qd) + spread(near_qd)
    key_value_grad = pl.pallas_call(
        functools.partial(key_kernel, count, slots),
        out_shape=jax.ShapeDtypeStruct(own_kv.shape, jnp.bfloat16),
        in_specs=[SMEM] + [VMEM] * (4 + count - 1 + 3),
        out_specs=VMEM,
        cost_estimate=cost(rows, width, count),
    )(index, choose, own_kv, own_q, own_do, *qd_blocks, row_stats, far_stats, near_stats)
    return attended[None, None], query_grad[None, None], key_value_grad[None, None]


def solution(mesh):
    placed = (
        P("gx", "gy", None, None),
        P("gx", "gy", None, None, None),
        P("gx", "gy", None, None),
        P("gx", "gy", None),
    )
    return jax.shard_map(
        per_device,
        mesh=mesh,
        in_specs=placed,
        out_specs=(
            P("gx", "gy", None, None),
            P("gx", "gy", None, None),
            P("gx", "gy", None, None, None),
        ),
        check_vma=False,
    )
```

profile of v0, /device:TPU:1, one launch (start us, length us, event | category | flops | bytes accessed | tf_op | source)
XLA Modules:
  0.0 85.7 jit_solution(2358772615799790940)
XLA Ops:
  0.6 0.1 collective-permute-start
  0.8 2.7 %collective-permute-start.1 = (bf16[2,128,768]{2,1,0:T(8,128)(2,1)}, bf16[2,128,768]{2,1,0:T(8,128)(2,1)S(1)}, u32[]{:S(2)}, u32[]{:S(2)}) collective-permute-start(bf16[2,128,768]{2,1,0:T(8,128)(2,1)} %bitcast.22), channel_id=1, source_target_pairs={{0,16},{8,24},{16,0},{24,8},{1,17},{9,25},{17,1},{25,9},{2,18},{10... | collective-permute-start | bytes 1179656 | tf_op jit(solution)/shard_map/ppermute | solution.py:27
  3.4 0.7 collective-permute-start.3
  4.1 3.8 %collective-permute-start.6 = (bf16[2,128,768]{2,1,0:T(8,128)(2,1)}, bf16[2,128,768]{2,1,0:T(8,128)(2,1)S(1)}, u32[]{:S(2)}, u32[]{:S(2)}) collective-permute-start(bf16[2,128,768]{2,1,0:T(8,128)(2,1)} %bitcast.24), channel_id=1, source_target_pairs={{0,1},{1,0},{2,3},{3,2},{4,5},{5,4},{6,7},{7,6},{8,9},{9,8},{10,11... | collective-permute-start | bytes 1179656 | tf_op jit(solution)/shard_map/ppermute | solution.py:23
  7.9 1.1 %pad_maximum_fusion = bf16[2,128,768]{2,1,0:T(8,128)(2,1)S(1)} fusion(bf16[1,128,768]{2,1,0:T(8,128)(2,1)} %bitcast.18, bf16[1,128,768]{2,1,0:T(8,128)(2,1)} %bitcast.15), kind=kLoop, calls=%fused_computation | loop fusion | flops 196608 | bytes 786432 | tf_op jit(solution)/shard_map/stack | solution.py:184
  8.9 1.0 %collective-permute-start.9 = (bf16[2,128,768]{2,1,0:T(8,128)(2,1)S(1)}, bf16[2,128,768]{2,1,0:T(8,128)(2,1)S(1)}, u32[]{:S(2)}, u32[]{:S(2)}) collective-permute-start(bf16[2,128,768]{2,1,0:T(8,128)(2,1)S(1)} %pad_maximum_fusion), channel_id=1, source_target_pairs={{0,8},{8,0},{16,24},{24,16},{1,9},{9,1},{17,25},{25,17},{2,10},{10... | collective-permute-start | bytes 1179656 | tf_op jit(solution)/shard_map/ppermute | solution.py:23
  10.1 0.3 collective-permute-start.10
  10.4 2.6 %collective-permute-done.1.refs_3_ = bf16[2,128,768]{2,1,0:T(8,128)(2,1)S(1)} collective-permute-done((bf16[2,128,768]{2,1,0:T(8,128)(2,1)}, bf16[2,128,768]{2,1,0:T(8,128)(2,1)S(1)}, u32[]{:S(2)}, u32[]{:S(2)}) %collective-permute-start.1) | collective-permute-done | bytes 393248 | tf_op jit(solution)/shard_map/ppermute | solution.py:27
  13.0 0.7 collective-permute-start.12
  13.7 4.3 %collective-permute-start.15 = (bf16[2,128,768]{2,1,0:T(8,128)(2,1)S(1)}, bf16[2,128,768]{2,1,0:T(8,128)(2,1)S(1)}, u32[]{:S(2)}, u32[]{:S(2)}) collective-permute-start(bf16[2,128,768]{2,1,0:T(8,128)(2,1)S(1)} %pad_maximum_fusion), channel_id=1, source_target_pairs={{0,1},{1,0},{2,3},{3,2},{4,5},{5,4},{6,7},{7,6},{8,9},{9,8},{10,11... | collective-permute-start | bytes 1179656 | tf_op jit(solution)/shard_map/ppermute | solution.py:23
  18.1 15.4 %collective-permute-done.6.refs_7_ = bf16[2,128,768]{2,1,0:T(8,128)(2,1)S(1)} collective-permute-done((bf16[2,128,768]{2,1,0:T(8,128)(2,1)}, bf16[2,128,768]{2,1,0:T(8,128)(2,1)S(1)}, u32[]{:S(2)}, u32[]{:S(2)}) %collective-permute-start.6) | collective-permute-done | bytes 393248 | tf_op jit(solution)/shard_map/ppermute | solution.py:23
  33.5 0.6 collective-permute-start.2
  34.1 0.7 fusion.choose_ref
  34.8 0.7 copy-done.20
  35.4 0.2 select_reduce_fusion
  35.6 2.5 %collective-permute-start.5 = (bf16[2,128,768]{2,1,0:T(8,128)(2,1)S(1)}, bf16[2,128,768]{2,1,0:T(8,128)(2,1)S(1)}, u32[]{:S(2)}, u32[]{:S(2)}) collective-permute-start(bf16[2,128,768]{2,1,0:T(8,128)(2,1)S(1)} %collective-permute-done.3.refs_4_), channel_id=1, source_target_pairs={{8,16},{16,8},{9,17},{17,9},{10,18},{18,10},{11,19},{19,11},{12,20... | collective-permute-start | bytes 1179656 | tf_op jit(solution)/shard_map/ppermute | solution.py:23
  38.2 3.5 %collective-permute-done.15.refs_6_ = bf16[2,128,768]{2,1,0:T(8,128)(2,1)S(1)} collective-permute-done((bf16[2,128,768]{2,1,0:T(8,128)(2,1)S(1)}, bf16[2,128,768]{2,1,0:T(8,128)(2,1)S(1)}, u32[]{:S(2)}, u32[]{:S(2)}) %collective-permute-start.15) | collective-permute-done | bytes 393248 | tf_op jit(solution)/shard_map/ppermute | solution.py:23
  41.8 2.5 %collective-permute-start.8 = (bf16[2,128,768]{2,1,0:T(8,128)(2,1)S(1)}, bf16[2,128,768]{2,1,0:T(8,128)(2,1)S(1)}, u32[]{:S(2)}, u32[]{:S(2)}) collective-permute-start(bf16[2,128,768]{2,1,0:T(8,128)(2,1)S(1)} %collective-permute-done.6.refs_7_), channel_id=1, source_target_pairs={{8,16},{16,8},{9,17},{17,9},{10,18},{18,10},{11,19},{19,11},{12,20... | collective-permute-start | bytes 1179656 | tf_op jit(solution)/shard_map/ppermute | solution.py:23
  44.3 0.6 or_select_fusion.bias_ref
  44.9 0.5 collective-permute-start.13
  45.5 3.0 %collective-permute-start.14 = (bf16[2,128,768]{2,1,0:T(8,128)(2,1)S(1)}, bf16[2,128,768]{2,1,0:T(8,128)(2,1)S(1)}, u32[]{:S(2)}, u32[]{:S(2)}) collective-permute-start(bf16[2,128,768]{2,1,0:T(8,128)(2,1)S(1)} %collective-permute-done.12.refs_3_), channel_id=1, source_target_pairs={{8,16},{16,8},{9,17},{17,9},{10,18},{18,10},{11,19},{19,11},{12,20... | collective-permute-start | bytes 1179656 | tf_op jit(solution)/shard_map/ppermute | solution.py:23
  48.7 2.2 %collective-permute-done.8.refs_9_ = bf16[2,128,768]{2,1,0:T(8,128)(2,1)S(1)} collective-permute-done((bf16[2,128,768]{2,1,0:T(8,128)(2,1)S(1)}, bf16[2,128,768]{2,1,0:T(8,128)(2,1)S(1)}, u32[]{:S(2)}, u32[]{:S(2)}) %collective-permute-start.8) | collective-permute-done | bytes 393248 | tf_op jit(solution)/shard_map/ppermute | solution.py:23
  50.9 2.5 %collective-permute-start.17 = (bf16[2,128,768]{2,1,0:T(8,128)(2,1)S(1)}, bf16[2,128,768]{2,1,0:T(8,128)(2,1)S(1)}, u32[]{:S(2)}, u32[]{:S(2)}) collective-permute-start(bf16[2,128,768]{2,1,0:T(8,128)(2,1)S(1)} %collective-permute-done.15.refs_6_), channel_id=1, source_target_pairs={{8,16},{16,8},{9,17},{17,9},{10,18},{18,10},{11,19},{19,11},{12,20... | collective-permute-start | bytes 1179656 | tf_op jit(solution)/shard_map/ppermute | solution.py:23
  53.4 0.6 broadcast_in_dim.57.flags_ref
  54.0 10.5 %shard_map.67 = (bf16[128,768]{1,0:T(8,128)(2,1)}, bf16[128,768]{1,0:T(8,128)(2,1)}, f32[32,128]{1,0:T(8,128)}) custom-call(f32[10]{0:T(128)} %or_select_fusion.bias_ref, bf16[128,768]{1,0:T(8,128)(2,1)} %bitcast.16, bf16[128,768]{1,0:T(8,128)(2,1)} %bitcast.19, f32[8,128]{1,0:T(8,128)} %broadcast_in_dim.57.flags_ref, bf16[2,128,768]{2,1,0:T(8,128)(2,1)} %bitcast.25, ...), custom_call_target="tpu_custom_call" | custom-call | flops 1006632960 | bytes 5111808 | tf_op jit(solution)/shard_map/pallas_call | solution.py:217
  64.6 5.0 %all-gather = f32[128,128]{1,0:T(8,128)S(1)} all-gather(f32[32,128]{1,0:T(8,128)} %get-tuple-element.8), channel_id=2, replica_groups=mesh['gx'=4,'gy'=8] {'gx'}, dimensions={0}, use_global_device_ids=true | all-gather | bytes 81920 | tf_op jit(solution)/shard_map/all_gather | solution.py:229
  69.6 0.8 collective-permute-start.18
  70.5 4.8 %collective-permute-start.19 = (f32[4,32,128]{2,1,0:T(8,128)S(1)}, f32[4,32,128]{2,1,0:T(8,128)S(1)}, u32[]{:S(2)}, u32[]{:S(2)}) collective-permute-start(f32[4,32,128]{2,1,0:T(8,128)S(1)} %bitcast.29), channel_id=1, source_target_pairs={{0,1},{1,0},{2,3},{3,2},{4,5},{5,4},{6,7},{7,6},{8,9},{9,8},{10,11... | collective-permute-start | bytes 196616 | tf_op jit(solution)/shard_map/ppermute | solution.py:23
  75.2 0.6 broadcast_clamp_fusion.index_ref
  75.9 1.9 %collective-permute-done.19.refs_11_ = f32[4,32,128]{2,1,0:T(8,128)S(1)} collective-permute-done((f32[4,32,128]{2,1,0:T(8,128)S(1)}, f32[4,32,128]{2,1,0:T(8,128)S(1)}, u32[]{:S(2)}, u32[]{:S(2)}) %collective-permute-start.19) | collective-permute-done | bytes 65568 | tf_op jit(solution)/shard_map/ppermute | solution.py:23
  77.8 0.6 copy-done.19
  78.4 7.3 %shard_map.68 = bf16[2,128,768]{2,1,0:T(8,128)(2,1)} custom-call(s32[10]{0:T(128)} %broadcast_clamp_fusion.index_ref, f32[10,128]{1,0:T(8,128)} %fusion.choose_ref, bf16[2,128,768]{2,1,0:T(8,128)(2,1)} %bitcast.26, bf16[128,768]{1,0:T(8,128)(2,1)} %bitcast.17, bf16[128,768]{1,0:T(8,128)(2,1)} %bitcast.20, bf16[2,128,768]{2,1,0:T(8,128)(2,1)} %copy-done, ...), custom_call_target="tpu_custom_call" | custom-call | flops 1006632960 | bytes 5111808 | tf_op jit(solution)/shard_map/pallas_call | solution.py:232
  (66 shorter events, 0.5 us)
Async XLA Ops:
  0.6 9.5 %collective-permute-start = (bf16[2,128,768]{2,1,0:T(8,128)(2,1)}, bf16[2,128,768]{2,1,0:T(8,128)(2,1)}, u32[]{:S(2)}, u32[]{:S(2)}) collective-permute-start(bf16[2,128,768]{2,1,0:T(8,128)(2,1)} %bitcast.21), channel_id=1, source_target_pairs={{0,8},{8,0},{16,24},{24,16},{1,9},{9,1},{17,25},{25,17},{2,10},{10... | collective-permute-start | bytes 1179656 | tf_op jit(solution)/shard_map/ppermute | solution.py:23
  0.8 12.3 %collective-permute-start.1 = (bf16[2,128,768]{2,1,0:T(8,128)(2,1)}, bf16[2,128,768]{2,1,0:T(8,128)(2,1)S(1)}, u32[]{:S(2)}, u32[]{:S(2)}) collective-permute-start(bf16[2,128,768]{2,1,0:T(8,128)(2,1)} %bitcast.22), channel_id=1, source_target_pairs={{0,16},{8,24},{16,0},{24,8},{1,17},{9,25},{17,1},{25,9},{2,18},{10... | collective-permute-start | bytes 1179656 | tf_op jit(solution)/shard_map/ppermute | solution.py:27
  3.4 10.3 %collective-permute-start.3 = (bf16[2,128,768]{2,1,0:T(8,128)(2,1)}, bf16[2,128,768]{2,1,0:T(8,128)(2,1)S(1)}, u32[]{:S(2)}, u32[]{:S(2)}) collective-permute-start(bf16[2,128,768]{2,1,0:T(8,128)(2,1)} %bitcast.23), channel_id=1, source_target_pairs={{1,2},{2,1},{3,4},{4,3},{5,6},{6,5},{9,10},{10,9},{11,12},{12,11},... | collective-permute-start | bytes 1179656 | tf_op jit(solution)/shard_map/ppermute | solution.py:23
  4.1 29.3 %collective-permute-start.6 = (bf16[2,128,768]{2,1,0:T(8,128)(2,1)}, bf16[2,128,768]{2,1,0:T(8,128)(2,1)S(1)}, u32[]{:S(2)}, u32[]{:S(2)}) collective-permute-start(bf16[2,128,768]{2,1,0:T(8,128)(2,1)} %bitcast.24), channel_id=1, source_target_pairs={{0,1},{1,0},{2,3},{3,2},{4,5},{5,4},{6,7},{7,6},{8,9},{9,8},{10,11... | collective-permute-start | bytes 1179656 | tf_op jit(solution)/shard_map/ppermute | solution.py:23
  8.9 25.1 %collective-permute-start.9 = (bf16[2,128,768]{2,1,0:T(8,128)(2,1)S(1)}, bf16[2,128,768]{2,1,0:T(8,128)(2,1)S(1)}, u32[]{:S(2)}, u32[]{:S(2)}) collective-permute-start(bf16[2,128,768]{2,1,0:T(8,128)(2,1)S(1)} %pad_maximum_fusion), channel_id=1, source_target_pairs={{0,8},{8,0},{16,24},{24,16},{1,9},{9,1},{17,25},{25,17},{2,10},{10... | collective-permute-start | bytes 1179656 | tf_op jit(solution)/shard_map/ppermute | solution.py:23
  10.1 25.5 %collective-permute-start.10 = (bf16[2,128,768]{2,1,0:T(8,128)(2,1)S(1)}, bf16[2,128,768]{2,1,0:T(8,128)(2,1)S(1)}, u32[]{:S(2)}, u32[]{:S(2)}) collective-permute-start(bf16[2,128,768]{2,1,0:T(8,128)(2,1)S(1)} %pad_maximum_fusion), channel_id=1, source_target_pairs={{0,16},{8,24},{16,0},{24,8},{1,17},{9,25},{17,1},{25,9},{2,18},{10... | collective-permute-start | bytes 1179656 | tf_op jit(solution)/shard_map/ppermute | solution.py:27
  13.0 31.9 %copy-start.9 = (bf16[2,128,768]{2,1,0:T(8,128)(2,1)}, bf16[2,128,768]{2,1,0:T(8,128)(2,1)S(1)}, u32[]{:S(2)}) copy-start(bf16[2,128,768]{2,1,0:T(8,128)(2,1)S(1)} %collective-permute-done.1.refs_3_) | copy-start | bytes 1179652
  13.0 25.1 %collective-permute-start.12 = (bf16[2,128,768]{2,1,0:T(8,128)(2,1)S(1)}, bf16[2,128,768]{2,1,0:T(8,128)(2,1)S(1)}, u32[]{:S(2)}, u32[]{:S(2)}) collective-permute-start(bf16[2,128,768]{2,1,0:T(8,128)(2,1)S(1)} %pad_maximum_fusion), channel_id=1, source_target_pairs={{1,2},{2,1},{3,4},{4,3},{5,6},{6,5},{9,10},{10,9},{11,12},{12,11},... | collective-permute-start | bytes 1179656 | tf_op jit(solution)/shard_map/ppermute | solution.py:23
  13.7 31.8 %copy-start.10 = (bf16[2,128,768]{2,1,0:T(8,128)(2,1)}, bf16[2,128,768]{2,1,0:T(8,128)(2,1)S(1)}, u32[]{:S(2)}) copy-start(bf16[2,128,768]{2,1,0:T(8,128)(2,1)S(1)} %collective-permute-done.3.refs_4_) | copy-start | bytes 1179652
  13.7 28.0 %collective-permute-start.15 = (bf16[2,128,768]{2,1,0:T(8,128)(2,1)S(1)}, bf16[2,128,768]{2,1,0:T(8,128)(2,1)S(1)}, u32[]{:S(2)}, u32[]{:S(2)}) collective-permute-start(bf16[2,128,768]{2,1,0:T(8,128)(2,1)S(1)} %pad_maximum_fusion), channel_id=1, source_target_pairs={{0,1},{1,0},{2,3},{3,2},{4,5},{5,4},{6,7},{7,6},{8,9},{9,8},{10,11... | collective-permute-start | bytes 1179656 | tf_op jit(solution)/shard_map/ppermute | solution.py:23
  33.5 15.2 %copy-start.11 = (bf16[2,128,768]{2,1,0:T(8,128)(2,1)}, bf16[2,128,768]{2,1,0:T(8,128)(2,1)S(1)}, u32[]{:S(2)}) copy-start(bf16[2,128,768]{2,1,0:T(8,128)(2,1)S(1)} %collective-permute-done.6.refs_7_) | copy-start | bytes 1179652
  33.5 11.4 %collective-permute-start.2 = (bf16[2,128,768]{2,1,0:T(8,128)(2,1)S(1)}, bf16[2,128,768]{2,1,0:T(8,128)(2,1)S(1)}, u32[]{:S(2)}, u32[]{:S(2)}) collective-permute-start(bf16[2,128,768]{2,1,0:T(8,128)(2,1)S(1)} %collective-permute-done.1.refs_3_), channel_id=1, source_target_pairs={{0,8},{8,0},{16,24},{24,16},{1,9},{9,1},{17,25},{25,17},{2,10},{10... | collective-permute-start | bytes 1179656 | tf_op jit(solution)/shard_map/ppermute | solution.py:23
  34.0 30.5 %copy-start = (bf16[2,128,768]{2,1,0:T(8,128)(2,1)}, bf16[2,128,768]{2,1,0:T(8,128)(2,1)S(1)}, u32[]{:S(2)}) copy-start(bf16[2,128,768]{2,1,0:T(8,128)(2,1)S(1)} %collective-permute-done.9.refs_0_) | copy-start | bytes 1179652
  34.0 10.9 %collective-permute-start.4 = (bf16[2,128,768]{2,1,0:T(8,128)(2,1)S(1)}, bf16[2,128,768]{2,1,0:T(8,128)(2,1)S(1)}, u32[]{:S(2)}, u32[]{:S(2)}) collective-permute-start(bf16[2,128,768]{2,1,0:T(8,128)(2,1)S(1)} %collective-permute-done.3.refs_4_), channel_id=1, source_target_pairs={{0,8},{8,0},{16,24},{24,16},{1,9},{9,1},{17,25},{25,17},{2,10},{10... | collective-permute-start | bytes 1179656 | tf_op jit(solution)/shard_map/ppermute | solution.py:23
  35.6 28.9 %copy-start.1 = (bf16[2,128,768]{2,1,0:T(8,128)(2,1)}, bf16[2,128,768]{2,1,0:T(8,128)(2,1)S(1)}, u32[]{:S(2)}) copy-start(bf16[2,128,768]{2,1,0:T(8,128)(2,1)S(1)} %collective-permute-done.10.refs_2_) | copy-start | bytes 1179652
  35.6 9.9 %collective-permute-start.5 = (bf16[2,128,768]{2,1,0:T(8,128)(2,1)S(1)}, bf16[2,128,768]{2,1,0:T(8,128)(2,1)S(1)}, u32[]{:S(2)}, u32[]{:S(2)}) collective-permute-start(bf16[2,128,768]{2,1,0:T(8,128)(2,1)S(1)} %collective-permute-done.3.refs_4_), channel_id=1, source_target_pairs={{8,16},{16,8},{9,17},{17,9},{10,18},{18,10},{11,19},{19,11},{12,20... | collective-permute-start | bytes 1179656 | tf_op jit(solution)/shard_map/ppermute | solution.py:23
  38.1 26.4 %copy-start.2 = (bf16[2,128,768]{2,1,0:T(8,128)(2,1)}, bf16[2,128,768]{2,1,0:T(8,128)(2,1)S(1)}, u32[]{:S(2)}) copy-start(bf16[2,128,768]{2,1,0:T(8,128)(2,1)S(1)} %collective-permute-done.12.refs_3_) | copy-start | bytes 1179652
  38.1 10.4 %collective-permute-start.7 = (bf16[2,128,768]{2,1,0:T(8,128)(2,1)S(1)}, bf16[2,128,768]{2,1,0:T(8,128)(2,1)S(1)}, u32[]{:S(2)}, u32[]{:S(2)}) collective-permute-start(bf16[2,128,768]{2,1,0:T(8,128)(2,1)S(1)} %collective-permute-done.6.refs_7_), channel_id=1, source_target_pairs={{0,8},{8,0},{16,24},{24,16},{1,9},{9,1},{17,25},{25,17},{2,10},{10... | collective-permute-start | bytes 1179656 | tf_op jit(solution)/shard_map/ppermute | solution.py:23
  41.8 22.8 %copy-start.3 = (bf16[2,128,768]{2,1,0:T(8,128)(2,1)}, bf16[2,128,768]{2,1,0:T(8,128)(2,1)S(1)}, u32[]{:S(2)}) copy-start(bf16[2,128,768]{2,1,0:T(8,128)(2,1)S(1)} %collective-permute-done.15.refs_6_) | copy-start | bytes 1179652
  41.8 9.1 %collective-permute-start.8 = (bf16[2,128,768]{2,1,0:T(8,128)(2,1)S(1)}, bf16[2,128,768]{2,1,0:T(8,128)(2,1)S(1)}, u32[]{:S(2)}, u32[]{:S(2)}) collective-permute-start(bf16[2,128,768]{2,1,0:T(8,128)(2,1)S(1)} %collective-permute-done.6.refs_7_), channel_id=1, source_target_pairs={{8,16},{16,8},{9,17},{17,9},{10,18},{18,10},{11,19},{19,11},{12,20... | collective-permute-start | bytes 1179656 | tf_op jit(solution)/shard_map/ppermute | solution.py:23
  44.9 24.7 %collective-permute-start.11 = (bf16[2,128,768]{2,1,0:T(8,128)(2,1)S(1)}, bf16[2,128,768]{2,1,0:T(8,128)(2,1)S(1)}, u32[]{:S(2)}, u32[]{:S(2)}) collective-permute-start(bf16[2,128,768]{2,1,0:T(8,128)(2,1)S(1)} %collective-permute-done.10.refs_2_), channel_id=1, source_target_pairs={{0,8},{8,0},{16,24},{24,16},{1,9},{9,1},{17,25},{25,17},{2,10},{10... | collective-permute-start | bytes 1179656 | tf_op jit(solution)/shard_map/ppermute | solution.py:23
  44.9 5.9 %copy-start.13 = (bf16[2,128,768]{2,1,0:T(8,128)(2,1)}, bf16[2,128,768]{2,1,0:T(8,128)(2,1)S(1)}, u32[]{:S(2)}) copy-start(bf16[2,128,768]{2,1,0:T(8,128)(2,1)S(1)} %collective-permute-done.4.refs_5_) | copy-start | bytes 1179652
  44.9 25.5 %collective-permute-start.13 = (bf16[2,128,768]{2,1,0:T(8,128)(2,1)S(1)}, bf16[2,128,768]{2,1,0:T(8,128)(2,1)S(1)}, u32[]{:S(2)}, u32[]{:S(2)}) collective-permute-start(bf16[2,128,768]{2,1,0:T(8,128)(2,1)S(1)} %collective-permute-done.12.refs_3_), channel_id=1, source_target_pairs={{0,8},{8,0},{16,24},{24,16},{1,9},{9,1},{17,25},{25,17},{2,10},{10... | collective-permute-start | bytes 1179656 | tf_op jit(solution)/shard_map/ppermute | solution.py:23
  45.5 7.9 %copy-start.14 = (bf16[2,128,768]{2,1,0:T(8,128)(2,1)}, bf16[2,128,768]{2,1,0:T(8,128)(2,1)S(1)}, u32[]{:S(2)}) copy-start(bf16[2,128,768]{2,1,0:T(8,128)(2,1)S(1)} %collective-permute-done.5.refs_6_) | copy-start | bytes 1179652
  45.5 30.3 %collective-permute-start.14 = (bf16[2,128,768]{2,1,0:T(8,128)(2,1)S(1)}, bf16[2,128,768]{2,1,0:T(8,128)(2,1)S(1)}, u32[]{:S(2)}, u32[]{:S(2)}) collective-permute-start(bf16[2,128,768]{2,1,0:T(8,128)(2,1)S(1)} %collective-permute-done.12.refs_3_), channel_id=1, source_target_pairs={{8,16},{16,8},{9,17},{17,9},{10,18},{18,10},{11,19},{19,11},{12,20... | collective-permute-start | bytes 1179656 | tf_op jit(solution)/shard_map/ppermute | solution.py:23
  48.6 27.3 %collective-permute-start.16 = (bf16[2,128,768]{2,1,0:T(8,128)(2,1)S(1)}, bf16[2,128,768]{2,1,0:T(8,128)(2,1)S(1)}, u32[]{:S(2)}, u32[]{:S(2)}) collective-permute-start(bf16[2,128,768]{2,1,0:T(8,128)(2,1)S(1)} %collective-permute-done.15.refs_6_), channel_id=1, source_target_pairs={{0,8},{8,0},{16,24},{24,16},{1,9},{9,1},{17,25},{25,17},{2,10},{10... | collective-permute-start | bytes 1179656 | tf_op jit(solution)/shard_map/ppermute | solution.py:23
  50.9 25.0 %collective-permute-start.17 = (bf16[2,128,768]{2,1,0:T(8,128)(2,1)S(1)}, bf16[2,128,768]{2,1,0:T(8,128)(2,1)S(1)}, u32[]{:S(2)}, u32[]{:S(2)}) collective-permute-start(bf16[2,128,768]{2,1,0:T(8,128)(2,1)S(1)} %collective-permute-done.15.refs_6_), channel_id=1, source_target_pairs={{8,16},{16,8},{9,17},{17,9},{10,18},{18,10},{11,19},{19,11},{12,20... | collective-permute-start | bytes 1179656 | tf_op jit(solution)/shard_map/ppermute | solution.py:23
  69.6 8.2 %copy-start.17 = (f32[128,128]{1,0:T(8,128)}, f32[128,128]{1,0:T(8,128)S(1)}, u32[]{:S(2)}) copy-start(f32[128,128]{1,0:T(8,128)S(1)} %all-gather) | copy-start | bytes 196612
  69.6 8.2 %copy-start.4 = (bf16[2,128,768]{2,1,0:T(8,128)(2,1)}, bf16[2,128,768]{2,1,0:T(8,128)(2,1)S(1)}, u32[]{:S(2)}) copy-start(bf16[2,128,768]{2,1,0:T(8,128)(2,1)S(1)} %collective-permute-done.11.refs_1_) | copy-start | bytes 1179652
  69.6 6.3 %collective-permute-start.18 = (f32[4,32,128]{2,1,0:T(8,128)S(1)}, f32[4,32,128]{2,1,0:T(8,128)S(1)}, u32[]{:S(2)}, u32[]{:S(2)}) collective-permute-start(f32[4,32,128]{2,1,0:T(8,128)S(1)} %bitcast.28), channel_id=1, source_target_pairs={{1,2},{2,1},{3,4},{4,3},{5,6},{6,5},{9,10},{10,9},{11,12},{12,11},... | collective-permute-start | bytes 196616 | tf_op jit(solution)/shard_map/ppermute | solution.py:23
  70.4 7.3 %copy-start.5 = (bf16[2,128,768]{2,1,0:T(8,128)(2,1)}, bf16[2,128,768]{2,1,0:T(8,128)(2,1)S(1)}, u32[]{:S(2)}) copy-start(bf16[2,128,768]{2,1,0:T(8,128)(2,1)S(1)} %collective-permute-done.13.refs_4_) | copy-start | bytes 1179652
  70.5 7.3 %collective-permute-start.19 = (f32[4,32,128]{2,1,0:T(8,128)S(1)}, f32[4,32,128]{2,1,0:T(8,128)S(1)}, u32[]{:S(2)}, u32[]{:S(2)}) collective-permute-start(f32[4,32,128]{2,1,0:T(8,128)S(1)} %bitcast.29), channel_id=1, source_target_pairs={{0,1},{1,0},{2,3},{3,2},{4,5},{5,4},{6,7},{7,6},{8,9},{9,8},{10,11... | collective-permute-start | bytes 196616 | tf_op jit(solution)/shard_map/ppermute | solution.py:23
  (9 other events, 20.1 us)
where the time goes:
time: 86.6 us; the launch traced here: 85.7 us
  starting transfers between devices  31 us (36%)
  waiting for transfers between devices  25.7 us (30%)
  Pallas kernels  17.8 us (21%)
  blocking collectives  4.98 us (6%)
  other arithmetic  3.11 us (4%)
  local copies, waits for them, and re-layouts  2.1 us (2%)
  between operations  0.99 us (1%)
    ppermute x18, starting transfers between devices, pair_swap(): return lax.ppermute(value, axis, pairs)  28.1 us
    ppermute x18, waiting for transfers between devices, pair_swap(): return lax.ppermute(value, axis, pairs)  23.1 us
    pallas_call x1, Pallas kernels, per_device(): pl.pallas_call(functools.partial(query_kernel, count), out_shape=(jax.Sha...  10.5 us
    pallas_call x1, Pallas kernels, per_device(): pl.pallas_call(functools.partial(key_kernel, count, slots), out_shape=jax...  7.32 us
    all_gather x1, blocking collectives, per_device(): row_stats = lax.all_gather(stats, 'gx')  4.98 us
    ppermute x2, starting transfers between devices, partner_swap(): lax.ppermute(value, 'gx', [(i, i ^ 1 << level) for i in range(lax.axis_si...  2.99 us
    ppermute x2, waiting for transfers between devices, partner_swap(): lax.ppermute(value, 'gx', [(i, i ^ 1 << level) for i in range(lax.axis_si...  2.61 us
  transfers between devices with their start and end apart: 20, of which 5 were waited for; matrix products, arithmetic and copies ran while one was open for 5% of the time, Pallas kernels for 12%

commit v1 on v0

--- a/solution.py
+++ b/solution.py
@@ -39,16 +39,17 @@
     return jnp.where(low, stacked[:rows], stacked[rows:])
 
 
-def query_kernel(count, bias_ref, q_ref, do_ref, flags_ref, *refs):
-    kv_refs = refs[:count]
-    att_ref, dq_ref, stats_ref = refs[count:]
+def query_kernel(count, first, last, bias_ref, q_ref, do_ref, flags_ref, *refs):
+    kv_refs, refs = refs[:count], refs[count:]
+    carried, (att_ref, dq_ref, stats_ref) = refs[:-3], refs[-3:]
     rows, width = q_ref.shape
     heads = width // E
     lane = lax.broadcasted_iota(jnp.int32, (rows, LANES), 1)
     low = lane < E
     stats = jnp.zeros((rows, LANES), jnp.float32)
-    for pair in range(width // LANES):
+    for pair in range(first, last):
         cols = slice(pair * LANES, (pair + 1) * LANES)
+        out_cols = cols if last * LANES == width else slice((pair - first) * LANES, (pair - first + 1) * LANES)
         grad = do_ref[:, cols]
         keys = jnp.concatenate([r[0, :, cols] for r in kv_refs], axis=0)
         values = jnp.concatenate([r[1, :, cols] for r in kv_refs], axis=0)
@@ -66,7 +67,7 @@
             raised.astype(jnp.bfloat16), values, preferred_element_type=jnp.float32
         )
         attended = join_heads(attended * inverse).astype(jnp.bfloat16)
-        att_ref[:, cols] = attended
+        att_ref[:, out_cols] = attended
         product = grad.astype(jnp.float32) * attended.astype(jnp.float32)
         delta = jnp.concatenate(
             [
@@ -80,19 +81,25 @@
         )
         score_grad = (raised * (prob_grad - delta)).astype(jnp.bfloat16)
         query_grad = jnp.dot(score_grad, keys, preferred_element_type=jnp.float32)
-        dq_ref[:, cols] = join_heads(query_grad * (inverse * SCALE)).astype(jnp.bfloat16)
+        dq_ref[:, out_cols] = join_heads(query_grad * (inverse * SCALE)).astype(jnp.bfloat16)
         level = largest + jnp.log2(totals)
         for half in range(2):
             head = 2 * pair + half
             part = slice(half * rows, (half + 1) * rows)
             stats = jnp.where(lane == head, level[part], stats)
             stats = jnp.where(lane == heads + head, delta[part], stats)
-    turned = stats.T
-    stats_ref[: 2 * heads] = turned[: 2 * heads]
+    turned = stats.T[: 2 * heads]
+    if carried:
+        att_in, dq_in, stats_in = carried
+        done = first * LANES
+        att_ref[:, :done] = att_in[...]
+        dq_ref[:, :done] = dq_in[...]
+        turned = turned + stats_in[: 2 * heads]
+    stats_ref[: 2 * heads] = turned
     stats_ref[2 * heads :] = flags_ref[...]
 
 
-def key_kernel(count, slots, index_ref, choose_ref, kv_ref, q_ref, do_ref, *refs):
+def key_kernel(count, slots, bases, index_ref, choose_ref, kv_ref, q_ref, do_ref, *refs):
     qd_refs = refs[: count - 1]
     stat_refs = refs[count - 1 : count + 2]
     out_ref = refs[count + 2]
@@ -118,8 +125,8 @@
 
     for pair in range(width // LANES):
         cols = slice(pair * LANES, (pair + 1) * LANES)
-        queries = jnp.concatenate([q_ref[:, cols]] + [r[0, :, cols] for r in qd_refs], axis=0)
-        grads = jnp.concatenate([do_ref[:, cols]] + [r[1, :, cols] for r in qd_refs], axis=0)
+        queries = jnp.concatenate([q_ref[:, cols]] + [r[o, :, cols] for r, o in zip(qd_refs, bases)], axis=0)
+        grads = jnp.concatenate([do_ref[:, cols]] + [r[o + 1, :, cols] for r, o in zip(qd_refs, bases)], axis=0)
         scores = lax.dot_general(
             split_heads(kv_ref[0, :, cols]),
             queries,
@@ -142,13 +149,26 @@
         out_ref[1, :, cols] = join_heads(value_grad).astype(jnp.bfloat16)
 
 
+def after(value, other):
+    return lax.optimization_barrier((value, other))[0]
+
+
+def both(a, b):
+    return lax.optimization_barrier((a, b))
+
+
+def on_chip(value):
+    return pltpu.with_memory_space_constraint(value, pltpu.MemorySpace.VMEM)
+
+
+PARAMS = pltpu.CompilerParams(vmem_limit_bytes=24 * 2**20)
 VMEM = pl.BlockSpec(memory_space=pltpu.VMEM)
 SMEM = pl.BlockSpec(memory_space=pltpu.SMEM)
 
 
 def cost(rows, width, count):
     return pl.CostEstimate(
-        flops=8 * rows * rows * width * count,
+        flops=64 * rows * rows * width * count,
         bytes_accessed=4 * rows * width * (count + 3),
         transcendentals=rows * rows * (width // E) * count,
     )
@@ -164,27 +184,48 @@
     side = 1 - 2 * (column % 2)
     turn = 1 - 2 * (line % 2)
 
-    def exchange_row(value):
-        pair = pair_swap(value, "gx", 0)
-        partners = [partner_swap(value, level) for level in range(1, levels + 1)]
+    def core_pair(value, tag):
+        with jax.named_scope(tag + "_X1"):
+            return pair_swap(value, "gx", 0)
+
+    def link_pair(value, tag):
+        with jax.named_scope(tag + "_X2"):
+            return pair_swap(value, "gx", 1)
+
+    def far(value, tag):
+        with jax.named_scope(tag + "_far"):
+            return pair_swap(value, "gy", 1)
+
+    def near(value, tag):
+        with jax.named_scope(tag + "_near"):
+            return pair_swap(value, "gy", 0)
+
+    def partners_of(value, tag):
+        with jax.named_scope(tag + "_PT"):
+            return [partner_swap(value, level) for level in range(1, levels + 1)]
+
+    def other_side(value, partners, tag):
         if columns == 4:
-            other = pair_swap(partners[0], "gx", 0)
-        else:
-            other = pair_swap(value, "gx", 1)
-        return [pair, other] + partners
-
-    def exchange_lines(value):
-        return pair_swap(value, "gy", 1), pair_swap(value, "gy", 0)
-
-    def spread(value):
-        return [value, pair_swap(value, "gx", 0), pair_swap(value, "gx", 1)]
-
-    far_kv, near_kv = exchange_lines(own_kv)
-    row_kv = exchange_row(own_kv)
-    own_qd = jnp.stack([own_q, own_do])
-    far_qd, near_qd = exchange_lines(own_qd)
-    row_qd = exchange_row(own_qd)
-    kv_blocks = [own_kv] + row_kv + spread(far_kv) + spread(near_kv)
+            return core_pair(partners[0], tag + "_PT")
+        return link_pair(value, tag)
+
+    kv_far = far(own_kv, "kv")
+    kv_near = near(own_kv, "kv")
+    kv_pair = core_pair(own_kv, "kv")
+    kv_partners = partners_of(after(own_kv, kv_pair), "kv")
+    ready = after(kv_far, kv_pair)
+    kv_far1, kv_far2 = core_pair(ready, "kvfar"), link_pair(ready, "kvfar")
+    kv_other = other_side(own_kv, kv_partners, "kv")
+    ready = after(kv_near, (kv_far1, kv_far2, kv_other))
+    kv_near1, kv_near2 = core_pair(ready, "kvnear"), link_pair(ready, "kvnear")
+    own_qd = jnp.stack([after(own_q, kv_far), own_do])
+    ready = after(own_qd, (kv_near, kv_far1, kv_far2, kv_other))
+    qd_far, qd_near = far(ready, "qd"), near(ready, "qd")
+    ready = after(own_qd, kv_near1)
+    qd_pair, qd_partners = core_pair(ready, "qd"), partners_of(ready, "qd")
+    kv_blocks = [own_kv, kv_pair, kv_other] + kv_partners
+    kv_blocks += [kv_far, kv_far1, kv_far2, kv_near, kv_near1, kv_near2]
+    kv_blocks = [on_chip(block) for block in kv_blocks]
 
     shift_x = [0, side, -side] + [0] * levels + [0, side, -side] * 2
     shift_y = [0] * (3 + levels) + [-turn] * 3 + [turn] * 3
@@ -214,26 +255,43 @@
     flags = jnp.where(lanes == LANES - 1, 1.0, flags)
     flags = jnp.broadcast_to(flags[None], (8, LANES))
 
-    attended, query_grad, stats = pl.pallas_call(
-        functools.partial(query_kernel, count),
-        out_shape=(
-            jax.ShapeDtypeStruct((rows, width), jnp.bfloat16),
-            jax.ShapeDtypeStruct((rows, width), jnp.bfloat16),
-            jax.ShapeDtypeStruct((2 * heads + 8, LANES), jnp.float32),
-        ),
-        in_specs=[SMEM] + [VMEM] * (3 + count),
-        out_specs=(VMEM, VMEM, VMEM),
-        cost_estimate=cost(rows, width, count),
-    )(bias, own_q, own_do, flags, *kv_blocks)
-
-    row_stats = lax.all_gather(stats, "gx")
-    far_stats, near_stats = exchange_lines(row_stats)
-    qd_blocks = row_qd + spread(far_qd) + spread(near_qd)
+    def query_side(first, last, carried):
+        full = last * LANES == width
+        part = jax.ShapeDtypeStruct(
+            (rows, width if full else (last - first) * LANES), jnp.bfloat16
+        )
+        return pl.pallas_call(
+            functools.partial(query_kernel, count, first, last),
+            out_shape=(
+                part,
+                part,
+                jax.ShapeDtypeStruct((2 * heads + 8, LANES), jnp.float32),
+            ),
+            in_specs=[SMEM] + [VMEM] * (3 + count + len(carried)),
+            out_specs=(VMEM, VMEM, VMEM),
+            compiler_params=PARAMS,
+            cost_estimate=cost(rows, (last - first) * LANES, count),
+        )(bias, own_q, own_do, flags, *kv_blocks, *carried)
+
+    attended, query_grad, stats = query_side(0, width // LANES, ())
+    stats, qd_far, qd_partners = lax.optimization_barrier((stats, qd_far, qd_partners))
+    qd_far1, qd_far2 = core_pair(qd_far, "qdfar"), link_pair(qd_far, "qdfar")
+    qd_other = other_side(own_qd, qd_partners, "qd")
+    with jax.named_scope("stats_row"):
+        row_stats = lax.all_gather(after(stats, (qd_far1, qd_other, qd_pair)), "gx")
+    ready = after(qd_near, row_stats)
+    qd_near1, qd_near2 = core_pair(ready, "qdnear"), link_pair(ready, "qdnear")
+    far_stats, near_stats = far(row_stats, "stats"), near(row_stats, "stats")
+    qd_blocks = [qd_pair, qd_other] + qd_partners
+    qd_blocks += [qd_far, qd_far1, qd_far2, qd_near, qd_near1, qd_near2]
+    qd_blocks = [on_chip(block) for block in qd_blocks]
+    bases = [0] * len(qd_blocks)
     key_value_grad = pl.pallas_call(
-        functools.partial(key_kernel, count, slots),
+        functools.partial(key_kernel, count, slots, bases),
         out_shape=jax.ShapeDtypeStruct(own_kv.shape, jnp.bfloat16),
         in_specs=[SMEM] + [VMEM] * (4 + count - 1 + 3),
         out_specs=VMEM,
+        compiler_params=PARAMS,
         cost_estimate=cost(rows, width, count),
     )(index, choose, own_kv, own_q, own_do, *qd_blocks, row_stats, far_stats, near_stats)
     return attended[None, None], query_grad[None, None], key_value_grad[None, None]

time: 86.6 us -> 72.5 us (0.84)
  starting transfers between devices: 31 us -> 24.9 us
  waiting for transfers between devices: 25.7 us -> 21.2 us
  Pallas kernels: 17.8 us -> 14.6 us
  blocking collectives: 4.98 us -> 7.95 us
  other arithmetic: 3.11 us -> 1.42 us
  local copies, waits for them, and re-layouts: 2.1 us -> 0.84 us
    ppermute x18, starting transfers between devices: 28.1 us -> 22.3 us  [pair_swap(): return lax.ppermute(value, axis, pairs)]
    ppermute x18, waiting for transfers between devices: 23.1 us -> 17.9 us  [pair_swap(): return lax.ppermute(value, axis, pairs)]
    pallas_call x2, Pallas kernels: 17.8 us -> 14.6 us  [the longest x1 8.94 us: query_side(): pl.pallas_call(functools.partial(query_kernel, count, first, last), out_s...]
    all_gather x1, blocking collectives: 4.98 us -> 7.95 us  [per_device(): row_stats = lax.all_gather(after(stats, (qd_far1, qd_other, qd_pair)), 'gx')]
  transfers between devices with their start and end apart: 20 -> 20, of which waited for: 5 -> 6; matrix products, arithmetic and copies ran while one was open for 5% -> 2% of each run, Pallas kernels for 12% -> 12%
where the time goes in v1:
time: 72.5 us; the launch traced here: 71.8 us
  starting transfers between devices  24.9 us (34%)
  waiting for transfers between devices  21.2 us (29%)
  Pallas kernels  14.6 us (20%)
  blocking collectives  7.95 us (11%)
  other arithmetic  1.42 us (2%)
  local copies, waits for them, and re-layouts  0.84 us (1%)
  between operations  0.84 us (1%)
    ppermute x18, starting transfers between devices, pair_swap(): return lax.ppermute(value, axis, pairs)  22.3 us
    ppermute x18, waiting for transfers between devices, pair_swap(): return lax.ppermute(value, axis, pairs)  17.9 us
    pallas_call x1, Pallas kernels, query_side(): pl.pallas_call(functools.partial(query_kernel, count, first, last), out_s...  8.94 us
    all_gather x1, blocking collectives, per_device(): row_stats = lax.all_gather(after(stats, (qd_far1, qd_other, qd_pair)), 'gx')  7.95 us
    pallas_call x1, Pallas kernels, per_device(): pl.pallas_call(functools.partial(key_kernel, count, slots, bases), out_sh...  5.71 us
    ppermute x2, waiting for transfers between devices, partner_swap(): lax.ppermute(value, 'gx', [(i, i ^ 1 << level) for i in range(lax.axis_si...  3.31 us
    ppermute x2, starting transfers between devices, partner_swap(): lax.ppermute(value, 'gx', [(i, i ^ 1 << level) for i in range(lax.axis_si...  2.65 us
  transfers between devices with their start and end apart: 20, of which 6 were waited for; matrix products, arithmetic and copies ran while one was open for 2% of the time, Pallas kernels for 12%

profile of v1, /device:TPU:1, one launch (start us, length us, event | category | flops | bytes accessed | tf_op | source)
XLA Modules:
  0.0 71.8 jit_solution(11368853322431117157)
XLA Ops:
  0.6 0.1 collective-permute-start
  0.8 0.7 collective-permute-start.3
  1.4 1.2 %collective-permute-done.refs_1_ = bf16[2,128,768]{2,1,0:T(8,128)(2,1)S(1)} collective-permute-done((bf16[2,128,768]{2,1,0:T(8,128)(2,1)}, bf16[2,128,768]{2,1,0:T(8,128)(2,1)S(1)}, u32[]{:S(2)}, u32[]{:S(2)}) %collective-permute-start) | collective-permute-done | bytes 393248 | tf_op jit(solution)/shard_map/kv_X1/ppermute | solution.py:23
  2.6 2.3 %collective-permute-start.1 = (bf16[2,128,768]{2,1,0:T(8,128)(2,1)}, bf16[2,128,768]{2,1,0:T(8,128)(2,1)S(1)}, u32[]{:S(2)}, u32[]{:S(2)}) collective-permute-start(bf16[2,128,768]{2,1,0:T(8,128)(2,1)} %bitcast.26), channel_id=1, source_target_pairs={{0,16},{8,24},{16,0},{24,8},{1,17},{9,25},{17,1},{25,9},{2,18},{10... | collective-permute-start | bytes 1179656 | tf_op jit(solution)/shard_map/kv_PT/ppermute | solution.py:27
  5.0 2.9 %collective-permute-start.6 = (bf16[2,128,768]{2,1,0:T(8,128)(2,1)}, bf16[2,128,768]{2,1,0:T(8,128)(2,1)S(1)}, u32[]{:S(2)}, u32[]{:S(2)}) collective-permute-start(bf16[2,128,768]{2,1,0:T(8,128)(2,1)} %bitcast.27), channel_id=1, source_target_pairs={{0,1},{1,0},{2,3},{3,2},{4,5},{5,4},{6,7},{7,6},{8,9},{9,8},{10,11... | collective-permute-start | bytes 1179656 | tf_op jit(solution)/shard_map/kv_near/ppermute | solution.py:23
  7.9 0.1 stack.37
  8.0 0.1 stack.34
  8.1 2.9 %collective-permute-start.5 = (bf16[2,128,768]{2,1,0:T(8,128)(2,1)S(1)}, bf16[2,128,768]{2,1,0:T(8,128)(2,1)S(1)}, u32[]{:S(2)}, u32[]{:S(2)}) collective-permute-start(bf16[2,128,768]{2,1,0:T(8,128)(2,1)S(1)} %collective-permute-done.3.refs_4_), channel_id=1, source_target_pairs={{8,16},{16,8},{9,17},{17,9},{10,18},{18,10},{11,19},{19,11},{12,20... | collective-permute-start | bytes 1179656 | tf_op jit(solution)/shard_map/kvfar_X2/ppermute | solution.py:23
  11.0 0.1 collective-permute-start.4
  11.1 3.3 %collective-permute-done.1.refs_3_ = bf16[2,128,768]{2,1,0:T(8,128)(2,1)S(1)} collective-permute-done((bf16[2,128,768]{2,1,0:T(8,128)(2,1)}, bf16[2,128,768]{2,1,0:T(8,128)(2,1)S(1)}, u32[]{:S(2)}, u32[]{:S(2)}) %collective-permute-start.1) | collective-permute-done | bytes 393248 | tf_op jit(solution)/shard_map/kv_PT/ppermute | solution.py:27
  14.4 1.1 %collective-permute-start.2 = (bf16[2,128,768]{2,1,0:T(8,128)(2,1)S(1)}, bf16[2,128,768]{2,1,0:T(8,128)(2,1)S(1)}, u32[]{:S(2)}, u32[]{:S(2)}) collective-permute-start(bf16[2,128,768]{2,1,0:T(8,128)(2,1)S(1)} %collective-permute-done.1.refs_3_), channel_id=1, source_target_pairs={{0,8},{8,0},{16,24},{24,16},{1,9},{9,1},{17,25},{25,17},{2,10},{10... | collective-permute-start | bytes 1179656 | tf_op jit(solution)/shard_map/kv_PT_X1/ppermute | solution.py:23
  15.4 0.6 copy-done.3
  16.1 0.2 select_reduce_fusion
  16.3 7.5 %collective-permute-done.6.refs_7_ = bf16[2,128,768]{2,1,0:T(8,128)(2,1)S(1)} collective-permute-done((bf16[2,128,768]{2,1,0:T(8,128)(2,1)}, bf16[2,128,768]{2,1,0:T(8,128)(2,1)S(1)}, u32[]{:S(2)}, u32[]{:S(2)}) %collective-permute-start.6) | collective-permute-done | bytes 393248 | tf_op jit(solution)/shard_map/kv_near/ppermute | solution.py:23
  23.8 3.5 %collective-permute-start.8 = (bf16[2,128,768]{2,1,0:T(8,128)(2,1)S(1)}, bf16[2,128,768]{2,1,0:T(8,128)(2,1)S(1)}, u32[]{:S(2)}, u32[]{:S(2)}) collective-permute-start(bf16[2,128,768]{2,1,0:T(8,128)(2,1)S(1)} %collective-permute-done.6.refs_7_), channel_id=1, source_target_pairs={{8,16},{16,8},{9,17},{17,9},{10,18},{18,10},{11,19},{19,11},{12,20... | collective-permute-start | bytes 1179656 | tf_op jit(solution)/shard_map/kvnear_X2/ppermute | solution.py:23
  27.5 1.1 %pad_maximum_fusion = bf16[2,128,768]{2,1,0:T(8,128)(2,1)S(1)} fusion(bf16[1,128,768]{2,1,0:T(8,128)(2,1)} %bitcast.18, bf16[1,128,768]{2,1,0:T(8,128)(2,1)} %bitcast.15), kind=kLoop, calls=%fused_computation | loop fusion | flops 196608 | bytes 786432 | tf_op jit(solution)/shard_map/stack | solution.py:221
  28.6 0.7 collective-permute-start.10
  29.3 0.3 collective-permute-start.11
  29.6 0.3 collective-permute-start.9
  29.9 4.0 %collective-permute-done.8.refs_9_ = bf16[2,128,768]{2,1,0:T(8,128)(2,1)S(1)} collective-permute-done((bf16[2,128,768]{2,1,0:T(8,128)(2,1)S(1)}, bf16[2,128,768]{2,1,0:T(8,128)(2,1)S(1)}, u32[]{:S(2)}, u32[]{:S(2)}) %collective-permute-start.8) | collective-permute-done | bytes 393248 | tf_op jit(solution)/shard_map/kvnear_X2/ppermute | solution.py:23
  34.0 8.9 %shard_map.67 = (bf16[128,768]{1,0:T(8,128)(2,1)}, bf16[128,768]{1,0:T(8,128)(2,1)}, f32[32,128]{1,0:T(8,128)S(1)}) custom-call(f32[10]{0:T(128)S(1)} %or_select_fusion.bias_ref, bf16[128,768]{1,0:T(8,128)(2,1)S(1)} %bitcast.16, bf16[128,768]{1,0:T(8,128)(2,1)S(1)} %bitcast.19, f32[8,128]{1,0:T(8,128)S(1)} %broadcast_in_dim.57.flags_ref, ...), custom_call_target="tpu_custom_call" | custom-call | flops 8053063680 | bytes 5111808 | tf_op jit(solution)/shard_map/pallas_call | solution.py:263
  42.9 0.5 collective-permute-start.13
  43.4 2.8 %collective-permute-start.15 = (bf16[2,128,768]{2,1,0:T(8,128)(2,1)S(1)}, bf16[2,128,768]{2,1,0:T(8,128)(2,1)S(1)}, u32[]{:S(2)}, u32[]{:S(2)}) collective-permute-start(bf16[2,128,768]{2,1,0:T(8,128)(2,1)S(1)} %pad_maximum_fusion), channel_id=1, source_target_pairs={{0,1},{1,0},{2,3},{3,2},{4,5},{5,4},{6,7},{7,6},{8,9},{9,8},{10,11... | collective-permute-start | bytes 1179656 | tf_op jit(solution)/shard_map/qd_near/ppermute | solution.py:23
  46.2 2.8 %collective-permute-start.14 = (bf16[2,128,768]{2,1,0:T(8,128)(2,1)S(1)}, bf16[2,128,768]{2,1,0:T(8,128)(2,1)S(1)}, u32[]{:S(2)}, u32[]{:S(2)}) collective-permute-start(bf16[2,128,768]{2,1,0:T(8,128)(2,1)S(1)} %collective-permute-done.10.refs_3_), channel_id=1, source_target_pairs={{8,16},{16,8},{9,17},{17,9},{10,18},{18,10},{11,19},{19,11},{12,20... | collective-permute-start | bytes 1179656 | tf_op jit(solution)/shard_map/qdfar_X2/ppermute | solution.py:23
  49.0 8.0 %all-gather = f32[128,128]{1,0:T(8,128)S(1)} all-gather(f32[32,128]{1,0:T(8,128)S(1)} %get-tuple-element.29), channel_id=2, replica_groups=mesh['gx'=4,'gy'=8] {'gx'}, dimensions={0}, use_global_device_ids=true | all-gather | bytes 81920 | tf_op jit(solution)/shard_map/stats_row/all_gather | solution.py:281
  57.0 2.2 %collective-permute-start.17 = (bf16[2,128,768]{2,1,0:T(8,128)(2,1)S(1)}, bf16[2,128,768]{2,1,0:T(8,128)(2,1)S(1)}, u32[]{:S(2)}, u32[]{:S(2)}) collective-permute-start(bf16[2,128,768]{2,1,0:T(8,128)(2,1)S(1)} %collective-permute-done.15.refs_6_), channel_id=1, source_target_pairs={{8,16},{16,8},{9,17},{17,9},{10,18},{18,10},{11,19},{19,11},{12,20... | collective-permute-start | bytes 1179656 | tf_op jit(solution)/shard_map/qdnear_X2/ppermute | solution.py:23
  59.3 0.1 fusion.choose_ref
  59.4 0.8 %collective-permute-start.19 = (f32[4,32,128]{2,1,0:T(8,128)S(1)}, f32[4,32,128]{2,1,0:T(8,128)S(1)}, u32[]{:S(2)}, u32[]{:S(2)}) collective-permute-start(f32[4,32,128]{2,1,0:T(8,128)S(1)} %bitcast.21), channel_id=1, source_target_pairs={{0,1},{1,0},{2,3},{3,2},{4,5},{5,4},{6,7},{7,6},{8,9},{9,8},{10,11... | collective-permute-start | bytes 196616 | tf_op jit(solution)/shard_map/stats_near/ppermute | solution.py:23
  60.1 0.8 %collective-permute-start.18 = (f32[4,32,128]{2,1,0:T(8,128)S(1)}, f32[4,32,128]{2,1,0:T(8,128)S(1)}, u32[]{:S(2)}, u32[]{:S(2)}) collective-permute-start(f32[4,32,128]{2,1,0:T(8,128)S(1)} %bitcast.22), channel_id=1, source_target_pairs={{1,2},{2,1},{3,4},{4,3},{5,6},{6,5},{9,10},{10,9},{11,12},{12,11},... | collective-permute-start | bytes 196616 | tf_op jit(solution)/shard_map/stats_far/ppermute | solution.py:23
  61.0 1.5 %collective-permute-done.19.refs_11_ = f32[4,32,128]{2,1,0:T(8,128)S(1)} collective-permute-done((f32[4,32,128]{2,1,0:T(8,128)S(1)}, f32[4,32,128]{2,1,0:T(8,128)S(1)}, u32[]{:S(2)}, u32[]{:S(2)}) %collective-permute-start.19) | collective-permute-done | bytes 65568 | tf_op jit(solution)/shard_map/stats_near/ppermute | solution.py:23
  62.5 3.6 %collective-permute-done.17.refs_8_ = bf16[2,128,768]{2,1,0:T(8,128)(2,1)S(1)} collective-permute-done((bf16[2,128,768]{2,1,0:T(8,128)(2,1)S(1)}, bf16[2,128,768]{2,1,0:T(8,128)(2,1)S(1)}, u32[]{:S(2)}, u32[]{:S(2)}) %collective-permute-start.17) | collective-permute-done | bytes 393248 | tf_op jit(solution)/shard_map/qdnear_X2/ppermute | solution.py:23
  66.1 5.7 %shard_map.68 = bf16[2,128,768]{2,1,0:T(8,128)(2,1)} custom-call(s32[10]{0:T(128)S(1)} %broadcast_clamp_fusion.index_ref, f32[10,128]{1,0:T(8,128)S(1)} %fusion.choose_ref, bf16[2,128,768]{2,1,0:T(8,128)(2,1)S(1)} %bitcast.29, bf16[128,768]{1,0:T(8,128)(2,1)S(1)} %bitcast.17, bf16[128,768]{1,0:T(8,128)(2,1)S(1)} %bitcast.20, ...), custom_call_target="tpu_custom_call" | custom-call | flops 8053063680 | bytes 5111808 | tf_op jit(solution)/shard_map/pallas_call | solution.py:289
  (32 shorter events, 0.2 us)
Async XLA Ops:
  0.6 2.0 %collective-permute-start = (bf16[2,128,768]{2,1,0:T(8,128)(2,1)}, bf16[2,128,768]{2,1,0:T(8,128)(2,1)S(1)}, u32[]{:S(2)}, u32[]{:S(2)}) collective-permute-start(bf16[2,128,768]{2,1,0:T(8,128)(2,1)} %bitcast.24), channel_id=1, source_target_pairs={{0,8},{8,0},{16,24},{24,16},{1,9},{9,1},{17,25},{25,17},{2,10},{10... | collective-permute-start | bytes 1179656 | tf_op jit(solution)/shard_map/kv_X1/ppermute | solution.py:23
  0.8 7.3 %collective-permute-start.3 = (bf16[2,128,768]{2,1,0:T(8,128)(2,1)}, bf16[2,128,768]{2,1,0:T(8,128)(2,1)S(1)}, u32[]{:S(2)}, u32[]{:S(2)}) collective-permute-start(bf16[2,128,768]{2,1,0:T(8,128)(2,1)} %bitcast.25), channel_id=1, source_target_pairs={{1,2},{2,1},{3,4},{4,3},{5,6},{6,5},{9,10},{10,9},{11,12},{12,11},... | collective-permute-start | bytes 1179656 | tf_op jit(solution)/shard_map/kv_far/ppermute | solution.py:23
  2.6 11.7 %collective-permute-start.1 = (bf16[2,128,768]{2,1,0:T(8,128)(2,1)}, bf16[2,128,768]{2,1,0:T(8,128)(2,1)S(1)}, u32[]{:S(2)}, u32[]{:S(2)}) collective-permute-start(bf16[2,128,768]{2,1,0:T(8,128)(2,1)} %bitcast.26), channel_id=1, source_target_pairs={{0,16},{8,24},{16,0},{24,8},{1,17},{9,25},{17,1},{25,9},{2,18},{10... | collective-permute-start | bytes 1179656 | tf_op jit(solution)/shard_map/kv_PT/ppermute | solution.py:27
  5.0 18.8 %collective-permute-start.6 = (bf16[2,128,768]{2,1,0:T(8,128)(2,1)}, bf16[2,128,768]{2,1,0:T(8,128)(2,1)S(1)}, u32[]{:S(2)}, u32[]{:S(2)}) collective-permute-start(bf16[2,128,768]{2,1,0:T(8,128)(2,1)} %bitcast.27), channel_id=1, source_target_pairs={{0,1},{1,0},{2,3},{3,2},{4,5},{5,4},{6,7},{7,6},{8,9},{9,8},{10,11... | collective-permute-start | bytes 1179656 | tf_op jit(solution)/shard_map/kv_near/ppermute | solution.py:23
  8.1 15.7 %collective-permute-start.5 = (bf16[2,128,768]{2,1,0:T(8,128)(2,1)S(1)}, bf16[2,128,768]{2,1,0:T(8,128)(2,1)S(1)}, u32[]{:S(2)}, u32[]{:S(2)}) collective-permute-start(bf16[2,128,768]{2,1,0:T(8,128)(2,1)S(1)} %collective-permute-done.3.refs_4_), channel_id=1, source_target_pairs={{8,16},{16,8},{9,17},{17,9},{10,18},{18,10},{11,19},{19,11},{12,20... | collective-permute-start | bytes 1179656 | tf_op jit(solution)/shard_map/kvfar_X2/ppermute | solution.py:23
  11.0 12.8 %collective-permute-start.4 = (bf16[2,128,768]{2,1,0:T(8,128)(2,1)S(1)}, bf16[2,128,768]{2,1,0:T(8,128)(2,1)S(1)}, u32[]{:S(2)}, u32[]{:S(2)}) collective-permute-start(bf16[2,128,768]{2,1,0:T(8,128)(2,1)S(1)} %collective-permute-done.3.refs_4_), channel_id=1, source_target_pairs={{0,8},{8,0},{16,24},{24,16},{1,9},{9,1},{17,25},{25,17},{2,10},{10... | collective-permute-start | bytes 1179656 | tf_op jit(solution)/shard_map/kvfar_X1/ppermute | solution.py:23
  14.4 9.4 %collective-permute-start.2 = (bf16[2,128,768]{2,1,0:T(8,128)(2,1)S(1)}, bf16[2,128,768]{2,1,0:T(8,128)(2,1)S(1)}, u32[]{:S(2)}, u32[]{:S(2)}) collective-permute-start(bf16[2,128,768]{2,1,0:T(8,128)(2,1)S(1)} %collective-permute-done.1.refs_3_), channel_id=1, source_target_pairs={{0,8},{8,0},{16,24},{24,16},{1,9},{9,1},{17,25},{25,17},{2,10},{10... | collective-permute-start | bytes 1179656 | tf_op jit(solution)/shard_map/kv_PT_X1/ppermute | solution.py:23
  15.4 0.7 copy-start.3
  23.8 10.2 %collective-permute-start.8 = (bf16[2,128,768]{2,1,0:T(8,128)(2,1)S(1)}, bf16[2,128,768]{2,1,0:T(8,128)(2,1)S(1)}, u32[]{:S(2)}, u32[]{:S(2)}) collective-permute-start(bf16[2,128,768]{2,1,0:T(8,128)(2,1)S(1)} %collective-permute-done.6.refs_7_), channel_id=1, source_target_pairs={{8,16},{16,8},{9,17},{17,9},{10,18},{18,10},{11,19},{19,11},{12,20... | collective-permute-start | bytes 1179656 | tf_op jit(solution)/shard_map/kvnear_X2/ppermute | solution.py:23
  27.3 2.0 %collective-permute-start.7 = (bf16[2,128,768]{2,1,0:T(8,128)(2,1)S(1)}, bf16[2,128,768]{2,1,0:T(8,128)(2,1)S(1)}, u32[]{:S(2)}, u32[]{:S(2)}) collective-permute-start(bf16[2,128,768]{2,1,0:T(8,128)(2,1)S(1)} %collective-permute-done.6.refs_7_), channel_id=1, source_target_pairs={{0,8},{8,0},{16,24},{24,16},{1,9},{9,1},{17,25},{25,17},{2,10},{10... | collective-permute-start | bytes 1179656 | tf_op jit(solution)/shard_map/kvnear_X1/ppermute | solution.py:23
  27.4 6.6 %copy-start = (bf16[1,1,128,768]{3,2,1,0:T(8,128)(2,1)S(1)}, bf16[1,1,128,768]{3,2,1,0:T(8,128)(2,1)}, u32[]{:S(2)}) copy-start(bf16[1,1,128,768]{3,2,1,0:T(8,128)(2,1)} %param.4) | copy-start | bytes 589828
  27.4 6.5 %copy-start.1 = (bf16[1,1,128,768]{3,2,1,0:T(8,128)(2,1)S(1)}, bf16[1,1,128,768]{3,2,1,0:T(8,128)(2,1)}, u32[]{:S(2)}) copy-start(bf16[1,1,128,768]{3,2,1,0:T(8,128)(2,1)} %param.6) | copy-start | bytes 589828
  27.4 6.5 %copy-start.2 = (bf16[1,1,2,128,768]{4,3,2,1,0:T(8,128)(2,1)S(1)}, bf16[1,1,2,128,768]{4,3,2,1,0:T(8,128)(2,1)}, u32[]{:S(2)}) copy-start(bf16[1,1,2,128,768]{4,3,2,1,0:T(8,128)(2,1)} %param.5) | copy-start | bytes 1179652
  28.6 14.3 %collective-permute-start.10 = (bf16[2,128,768]{2,1,0:T(8,128)(2,1)S(1)}, bf16[2,128,768]{2,1,0:T(8,128)(2,1)S(1)}, u32[]{:S(2)}, u32[]{:S(2)}) collective-permute-start(bf16[2,128,768]{2,1,0:T(8,128)(2,1)S(1)} %pad_maximum_fusion), channel_id=1, source_target_pairs={{1,2},{2,1},{3,4},{4,3},{5,6},{6,5},{9,10},{10,9},{11,12},{12,11},... | collective-permute-start | bytes 1179656 | tf_op jit(solution)/shard_map/qd_far/ppermute | solution.py:23
  29.3 13.6 %collective-permute-start.11 = (bf16[2,128,768]{2,1,0:T(8,128)(2,1)S(1)}, bf16[2,128,768]{2,1,0:T(8,128)(2,1)S(1)}, u32[]{:S(2)}, u32[]{:S(2)}) collective-permute-start(bf16[2,128,768]{2,1,0:T(8,128)(2,1)S(1)} %pad_maximum_fusion), channel_id=1, source_target_pairs={{0,16},{8,24},{16,0},{24,8},{1,17},{9,25},{17,1},{25,9},{2,18},{10... | collective-permute-start | bytes 1179656 | tf_op jit(solution)/shard_map/qd_PT/ppermute | solution.py:27
  29.6 19.4 %collective-permute-start.9 = (bf16[2,128,768]{2,1,0:T(8,128)(2,1)S(1)}, bf16[2,128,768]{2,1,0:T(8,128)(2,1)S(1)}, u32[]{:S(2)}, u32[]{:S(2)}) collective-permute-start(bf16[2,128,768]{2,1,0:T(8,128)(2,1)S(1)} %pad_maximum_fusion), channel_id=1, source_target_pairs={{0,8},{8,0},{16,24},{24,16},{1,9},{9,1},{17,25},{25,17},{2,10},{10... | collective-permute-start | bytes 1179656 | tf_op jit(solution)/shard_map/qd_X1/ppermute | solution.py:23
  42.9 6.1 %collective-permute-start.12 = (bf16[2,128,768]{2,1,0:T(8,128)(2,1)S(1)}, bf16[2,128,768]{2,1,0:T(8,128)(2,1)S(1)}, u32[]{:S(2)}, u32[]{:S(2)}) collective-permute-start(bf16[2,128,768]{2,1,0:T(8,128)(2,1)S(1)} %collective-permute-done.11.refs_2_), channel_id=1, source_target_pairs={{0,8},{8,0},{16,24},{24,16},{1,9},{9,1},{17,25},{25,17},{2,10},{10... | collective-permute-start | bytes 1179656 | tf_op jit(solution)/shard_map/qd_PT_X1/ppermute | solution.py:23
  42.9 6.1 %collective-permute-start.13 = (bf16[2,128,768]{2,1,0:T(8,128)(2,1)S(1)}, bf16[2,128,768]{2,1,0:T(8,128)(2,1)S(1)}, u32[]{:S(2)}, u32[]{:S(2)}) collective-permute-start(bf16[2,128,768]{2,1,0:T(8,128)(2,1)S(1)} %collective-permute-done.10.refs_3_), channel_id=1, source_target_pairs={{0,8},{8,0},{16,24},{24,16},{1,9},{9,1},{17,25},{25,17},{2,10},{10... | collective-permute-start | bytes 1179656 | tf_op jit(solution)/shard_map/qdfar_X1/ppermute | solution.py:23
  43.4 13.5 %collective-permute-start.15 = (bf16[2,128,768]{2,1,0:T(8,128)(2,1)S(1)}, bf16[2,128,768]{2,1,0:T(8,128)(2,1)S(1)}, u32[]{:S(2)}, u32[]{:S(2)}) collective-permute-start(bf16[2,128,768]{2,1,0:T(8,128)(2,1)S(1)} %pad_maximum_fusion), channel_id=1, source_target_pairs={{0,1},{1,0},{2,3},{3,2},{4,5},{5,4},{6,7},{7,6},{8,9},{9,8},{10,11... | collective-permute-start | bytes 1179656 | tf_op jit(solution)/shard_map/qd_near/ppermute | solution.py:23
  46.2 14.8 %collective-permute-start.14 = (bf16[2,128,768]{2,1,0:T(8,128)(2,1)S(1)}, bf16[2,128,768]{2,1,0:T(8,128)(2,1)S(1)}, u32[]{:S(2)}, u32[]{:S(2)}) collective-permute-start(bf16[2,128,768]{2,1,0:T(8,128)(2,1)S(1)} %collective-permute-done.10.refs_3_), channel_id=1, source_target_pairs={{8,16},{16,8},{9,17},{17,9},{10,18},{18,10},{11,19},{19,11},{12,20... | collective-permute-start | bytes 1179656 | tf_op jit(solution)/shard_map/qdfar_X2/ppermute | solution.py:23
  57.0 9.1 %collective-permute-start.17 = (bf16[2,128,768]{2,1,0:T(8,128)(2,1)S(1)}, bf16[2,128,768]{2,1,0:T(8,128)(2,1)S(1)}, u32[]{:S(2)}, u32[]{:S(2)}) collective-permute-start(bf16[2,128,768]{2,1,0:T(8,128)(2,1)S(1)} %collective-permute-done.15.refs_6_), channel_id=1, source_target_pairs={{8,16},{16,8},{9,17},{17,9},{10,18},{18,10},{11,19},{19,11},{12,20... | collective-permute-start | bytes 1179656 | tf_op jit(solution)/shard_map/qdnear_X2/ppermute | solution.py:23
  59.2 6.9 %collective-permute-start.16 = (bf16[2,128,768]{2,1,0:T(8,128)(2,1)S(1)}, bf16[2,128,768]{2,1,0:T(8,128)(2,1)S(1)}, u32[]{:S(2)}, u32[]{:S(2)}) collective-permute-start(bf16[2,128,768]{2,1,0:T(8,128)(2,1)S(1)} %collective-permute-done.15.refs_6_), channel_id=1, source_target_pairs={{0,8},{8,0},{16,24},{24,16},{1,9},{9,1},{17,25},{25,17},{2,10},{10... | collective-permute-start | bytes 1179656 | tf_op jit(solution)/shard_map/qdnear_X1/ppermute | solution.py:23
  59.4 3.1 %collective-permute-start.19 = (f32[4,32,128]{2,1,0:T(8,128)S(1)}, f32[4,32,128]{2,1,0:T(8,128)S(1)}, u32[]{:S(2)}, u32[]{:S(2)}) collective-permute-start(f32[4,32,128]{2,1,0:T(8,128)S(1)} %bitcast.21), channel_id=1, source_target_pairs={{0,1},{1,0},{2,3},{3,2},{4,5},{5,4},{6,7},{7,6},{8,9},{9,8},{10,11... | collective-permute-start | bytes 196616 | tf_op jit(solution)/shard_map/stats_near/ppermute | solution.py:23
  60.1 2.3 %collective-permute-start.18 = (f32[4,32,128]{2,1,0:T(8,128)S(1)}, f32[4,32,128]{2,1,0:T(8,128)S(1)}, u32[]{:S(2)}, u32[]{:S(2)}) collective-permute-start(f32[4,32,128]{2,1,0:T(8,128)S(1)} %bitcast.22), channel_id=1, source_target_pairs={{1,2},{2,1},{3,4},{4,3},{5,6},{6,5},{9,10},{10,9},{11,12},{12,11},... | collective-permute-start | bytes 196616 | tf_op jit(solution)/shard_map/stats_far/ppermute | solution.py:23

commit v2 on v1

--- a/solution.py
+++ b/solution.py
@@ -39,36 +39,46 @@
     return jnp.where(low, stacked[:rows], stacked[rows:])
 
 
-def query_kernel(count, first, last, bias_ref, q_ref, do_ref, flags_ref, *refs):
-    kv_refs, refs = refs[:count], refs[count:]
-    carried, (att_ref, dq_ref, stats_ref) = refs[:-3], refs[-3:]
+def per_lane(columns, lane, first, table):
+    rows = table.shape[0]
+    table = jnp.where(lane == first, columns[:rows], table)
+    return jnp.where(lane == first + 1, columns[rows:], table)
+
+
+def from_lanes(table, first):
+    return jnp.concatenate([table[:, first : first + 1], table[:, first + 1 : first + 2]], axis=0)
+
+
+def masked_scores(q_ref, kv_refs, bias_ref, start, cols):
+    rows = q_ref.shape[0]
+    keys = jnp.concatenate([r[0, :, cols] for r in kv_refs], axis=0)
+    scores = lax.dot_general(
+        split_heads(q_ref[:, cols]), keys, CONTRACT_LAST, preferred_element_type=jnp.float32
+    )
+    return keys, [
+        scores[:, b * rows : (b + 1) * rows] + bias_ref[start + b] for b in range(len(kv_refs))
+    ]
+
+
+def attend_kernel(count, bias_ref, q_ref, do_ref, flags_ref, *refs):
+    kv_refs, (att_ref, columns_ref, stats_ref) = refs[:count], refs[count:]
     rows, width = q_ref.shape
     heads = width // E
     lane = lax.broadcasted_iota(jnp.int32, (rows, LANES), 1)
     low = lane < E
-    stats = jnp.zeros((rows, LANES), jnp.float32)
-    for pair in range(first, last):
+    columns = jnp.zeros((rows, LANES), jnp.float32)
+    for pair in range(width // LANES):
         cols = slice(pair * LANES, (pair + 1) * LANES)
-        out_cols = cols if last * LANES == width else slice((pair - first) * LANES, (pair - first + 1) * LANES)
-        grad = do_ref[:, cols]
-        keys = jnp.concatenate([r[0, :, cols] for r in kv_refs], axis=0)
         values = jnp.concatenate([r[1, :, cols] for r in kv_refs], axis=0)
-        scores = lax.dot_general(
-            split_heads(q_ref[:, cols]), keys, CONTRACT_LAST, preferred_element_type=jnp.float32
-        )
-        scores = jnp.concatenate(
-            [scores[:, b * rows : (b + 1) * rows] + bias_ref[b] for b in range(count)], axis=1
-        )
+        _, scores = masked_scores(q_ref, kv_refs, bias_ref, 0, cols)
+        scores = jnp.concatenate(scores, axis=1)
         largest = jnp.max(scores, axis=1, keepdims=True) * FOLD
         raised = jnp.exp2(scores * FOLD - largest)
         totals = jnp.sum(raised, axis=1, keepdims=True)
-        inverse = 1.0 / totals
-        attended = jnp.dot(
-            raised.astype(jnp.bfloat16), values, preferred_element_type=jnp.float32
-        )
-        attended = join_heads(attended * inverse).astype(jnp.bfloat16)
-        att_ref[:, out_cols] = attended
-        product = grad.astype(jnp.float32) * attended.astype(jnp.float32)
+        sums = jnp.dot(raised.astype(jnp.bfloat16), values, preferred_element_type=jnp.float32)
+        attended = join_heads(sums * (1.0 / totals)).astype(jnp.bfloat16)
+        att_ref[:, cols] = attended
+        product = do_ref[:, cols].astype(jnp.float32) * attended.astype(jnp.float32)
         delta = jnp.concatenate(
             [
                 jnp.sum(jnp.where(low, product, 0.0), axis=1, keepdims=True),
@@ -76,27 +86,32 @@
             ],
             axis=0,
         )
+        columns = per_lane(largest + jnp.log2(totals), lane, 2 * pair, columns)
+        columns = per_lane(delta, lane, heads + 2 * pair, columns)
+    columns_ref[...] = columns
+    stats_ref[: 2 * heads] = columns.T[: 2 * heads]
+    stats_ref[2 * heads :] = flags_ref[...]
+
+
+def query_kernel(count, bias_ref, q_ref, do_ref, columns_ref, *refs):
+    kv_refs, dq_ref = refs[:count], refs[count]
+    rows, width = q_ref.shape
+    heads = width // E
+    columns = columns_ref[...]
+    for pair in range(width // LANES):
+        cols = slice(pair * LANES, (pair + 1) * LANES)
+        values = jnp.concatenate([r[1, :, cols] for r in kv_refs], axis=0)
+        keys, scores = masked_scores(q_ref, kv_refs, bias_ref, 0, cols)
+        weights = jnp.exp2(
+            jnp.concatenate(scores, axis=1) * FOLD - from_lanes(columns, 2 * pair)
+        )
         prob_grad = lax.dot_general(
-            split_heads(grad), values, CONTRACT_LAST, preferred_element_type=jnp.float32
-        )
-        score_grad = (raised * (prob_grad - delta)).astype(jnp.bfloat16)
+            split_heads(do_ref[:, cols]), values, CONTRACT_LAST, preferred_element_type=jnp.float32
+        )
+        delta = from_lanes(columns, heads + 2 * pair)
+        score_grad = (weights * (prob_grad - delta)).astype(jnp.bfloat16)
         query_grad = jnp.dot(score_grad, keys, preferred_element_type=jnp.float32)
-        dq_ref[:, out_cols] = join_heads(query_grad * (inverse * SCALE)).astype(jnp.bfloat16)
-        level = largest + jnp.log2(totals)
-        for half in range(2):
-            head = 2 * pair + half
-            part = slice(half * rows, (half + 1) * rows)
-            stats = jnp.where(lane == head, level[part], stats)
-            stats = jnp.where(lane == heads + head, delta[part], stats)
-    turned = stats.T[: 2 * heads]
-    if carried:
-        att_in, dq_in, stats_in = carried
-        done = first * LANES
-        att_ref[:, :done] = att_in[...]
-        dq_ref[:, :done] = dq_in[...]
-        turned = turned + stats_in[: 2 * heads]
-    stats_ref[: 2 * heads] = turned
-    stats_ref[2 * heads :] = flags_ref[...]
+        dq_ref[:, cols] = (join_heads(query_grad) * SCALE).astype(jnp.bfloat16)
 
 
 def key_kernel(count, slots, bases, index_ref, choose_ref, kv_ref, q_ref, do_ref, *refs):
@@ -161,17 +176,12 @@
     return pltpu.with_memory_space_constraint(value, pltpu.MemorySpace.VMEM)
 
 
-PARAMS = pltpu.CompilerParams(vmem_limit_bytes=24 * 2**20)
+PARAMS = pltpu.CompilerParams(vmem_limit_bytes=14 * 2**20)
 VMEM = pl.BlockSpec(memory_space=pltpu.VMEM)
 SMEM = pl.BlockSpec(memory_space=pltpu.SMEM)
 
 
-def cost(rows, width, count):
-    return pl.CostEstimate(
-        flops=64 * rows * rows * width * count,
-        bytes_accessed=4 * rows * width * (count + 3),
-        transcendentals=rows * rows * (width // E) * count,
-    )
+COST = pl.CostEstimate(flops=128, bytes_accessed=128, transcendentals=0)
 
 
 def per_device(queries, keys_values, out_grad, pattern):
@@ -213,16 +223,19 @@
     kv_near = near(own_kv, "kv")
     kv_pair = core_pair(own_kv, "kv")
     kv_partners = partners_of(after(own_kv, kv_pair), "kv")
-    ready = after(kv_far, kv_pair)
+    own_qd = jnp.stack([after(own_q, kv_pair), own_do])
+    qd_pair = core_pair(after(own_qd, kv_pair), "qd")
+    ready = after(kv_far, qd_pair)
     kv_far1, kv_far2 = core_pair(ready, "kvfar"), link_pair(ready, "kvfar")
     kv_other = other_side(own_kv, kv_partners, "kv")
+    qd_partners = partners_of(after(own_qd, kv_partners), "qd")
+    qd_far = far(after(own_qd, kv_far), "qd")
+    qd_near = near(after(own_qd, kv_far), "qd")
     ready = after(kv_near, (kv_far1, kv_far2, kv_other))
     kv_near1, kv_near2 = core_pair(ready, "kvnear"), link_pair(ready, "kvnear")
-    own_qd = jnp.stack([after(own_q, kv_far), own_do])
-    ready = after(own_qd, (kv_near, kv_far1, kv_far2, kv_other))
-    qd_far, qd_near = far(ready, "qd"), near(ready, "qd")
-    ready = after(own_qd, kv_near1)
-    qd_pair, qd_partners = core_pair(ready, "qd"), partners_of(ready, "qd")
+    ready = after(qd_far, kv_near1)
+    qd_far1, qd_far2 = core_pair(ready, "qdfar"), link_pair(ready, "qdfar")
+    qd_other = other_side(own_qd, qd_partners, "qd")
     kv_blocks = [own_kv, kv_pair, kv_other] + kv_partners
     kv_blocks += [kv_far, kv_far1, kv_far2, kv_near, kv_near1, kv_near2]
     kv_blocks = [on_chip(block) for block in kv_blocks]
@@ -255,33 +268,34 @@
     flags = jnp.where(lanes == LANES - 1, 1.0, flags)
     flags = jnp.broadcast_to(flags[None], (8, LANES))
 
-    def query_side(first, last, carried):
-        full = last * LANES == width
-        part = jax.ShapeDtypeStruct(
-            (rows, width if full else (last - first) * LANES), jnp.bfloat16
-        )
+    def call(kernel, inputs, outputs):
         return pl.pallas_call(
-            functools.partial(query_kernel, count, first, last),
-            out_shape=(
-                part,
-                part,
-                jax.ShapeDtypeStruct((2 * heads + 8, LANES), jnp.float32),
-            ),
-            in_specs=[SMEM] + [VMEM] * (3 + count + len(carried)),
-            out_specs=(VMEM, VMEM, VMEM),
+            kernel,
+            out_shape=outputs,
+            in_specs=[SMEM] + [VMEM] * (len(inputs) - 1),
+            out_specs=jax.tree.map(lambda _: VMEM, outputs),
             compiler_params=PARAMS,
-            cost_estimate=cost(rows, (last - first) * LANES, count),
-        )(bias, own_q, own_do, flags, *kv_blocks, *carried)
-
-    attended, query_grad, stats = query_side(0, width // LANES, ())
-    stats, qd_far, qd_partners = lax.optimization_barrier((stats, qd_far, qd_partners))
-    qd_far1, qd_far2 = core_pair(qd_far, "qdfar"), link_pair(qd_far, "qdfar")
-    qd_other = other_side(own_qd, qd_partners, "qd")
+            cost_estimate=COST,
+        )(*inputs)
+
+    wide = jax.ShapeDtypeStruct((rows, width), jnp.bfloat16)
+    table = jax.ShapeDtypeStruct((rows, LANES), jnp.float32)
+    bias = after(bias, qd_far1)
+    attended, columns_of, stats = call(
+        functools.partial(attend_kernel, count),
+        (bias, own_q, own_do, flags, *kv_blocks),
+        (wide, table, jax.ShapeDtypeStruct((2 * heads + 8, LANES), jnp.float32)),
+    )
     with jax.named_scope("stats_row"):
-        row_stats = lax.all_gather(after(stats, (qd_far1, qd_other, qd_pair)), "gx")
+        row_stats = lax.all_gather(after(stats, (qd_near, qd_other)), "gx")
     ready = after(qd_near, row_stats)
     qd_near1, qd_near2 = core_pair(ready, "qdnear"), link_pair(ready, "qdnear")
     far_stats, near_stats = far(row_stats, "stats"), near(row_stats, "stats")
+    query_grad = call(
+        functools.partial(query_kernel, count),
+        (bias, own_q, own_do, after(columns_of, row_stats), *kv_blocks),
+        wide,
+    )
     qd_blocks = [qd_pair, qd_other] + qd_partners
     qd_blocks += [qd_far, qd_far1, qd_far2, qd_near, qd_near1, qd_near2]
     qd_blocks = [on_chip(block) for block in qd_blocks]
@@ -292,7 +306,7 @@
         in_specs=[SMEM] + [VMEM] * (4 + count - 1 + 3),
         out_specs=VMEM,
         compiler_params=PARAMS,
-        cost_estimate=cost(rows, width, count),
+        cost_estimate=COST,
     )(index, choose, own_kv, own_q, own_do, *qd_blocks, row_stats, far_stats, near_stats)
     return attended[None, None], query_grad[None, None], key_value_grad[None, None]
 

time: 72.5 us -> 69.9 us (0.964)
  starting transfers between devices: 24.9 us -> 33.5 us
  waiting for transfers between devices: 21.2 us -> 13.2 us
  blocking collectives: 7.95 us -> 4.08 us
  Pallas kernels: 14.6 us -> 15.7 us
    ppermute x18, waiting for transfers between devices: 17.9 us -> 7.43 us  [pair_swap(): return lax.ppermute(value, axis, pairs)]
    ppermute x18, starting transfers between devices: 22.3 us -> 29.7 us  [pair_swap(): return lax.ppermute(value, axis, pairs)]
    all_gather x1, blocking collectives: 7.95 us -> 4.08 us  [per_device(): row_stats = lax.all_gather(after(stats, (qd_near, qd_other)), 'gx')]
    ppermute x2, waiting for transfers between devices: 3.31 us -> 5.81 us  [partner_swap(): lax.ppermute(value, 'gx', [(i, i ^ 1 << level) for i in range(lax.axis_si...]
    ppermute x2, starting transfers between devices: 2.65 us -> 3.79 us  [partner_swap(): lax.ppermute(value, 'gx', [(i, i ^ 1 << level) for i in range(lax.axis_si...]
    pallas_call x1 -> x2, Pallas kernels: 8.94 us -> 10 us  [call(): pl.pallas_call(kernel, out_shape=outputs, in_specs=[SMEM] + [VMEM] * (len...]
  transfers between devices with their start and end apart: 20 -> 20, of which waited for: 6 -> 4; matrix products, arithmetic and copies ran while one was open for 2% -> 2% of each run, Pallas kernels for 12% -> 14%
where the time goes in v2:
time: 69.9 us; the launch traced here: 69.7 us
  starting transfers between devices  33.5 us (48%)
  Pallas kernels  15.7 us (22%)
  waiting for transfers between devices  13.2 us (19%)
  blocking collectives  4.08 us (6%)
  other arithmetic  1.42 us (2%)
  local copies, waits for them, and re-layouts  0.94 us (1%)
  between operations  0.8 us (1%)
    ppermute x18, starting transfers between devices, pair_swap(): return lax.ppermute(value, axis, pairs)  29.7 us
    pallas_call x2, Pallas kernels, call(): pl.pallas_call(kernel, out_shape=outputs, in_specs=[SMEM] + [VMEM] * (len...  10 us
    ppermute x18, waiting for transfers between devices, pair_swap(): return lax.ppermute(value, axis, pairs)  7.43 us
    ppermute x2, waiting for transfers between devices, partner_swap(): lax.ppermute(value, 'gx', [(i, i ^ 1 << level) for i in range(lax.axis_si...  5.81 us
    pallas_call x1, Pallas kernels, per_device(): pl.pallas_call(functools.partial(key_kernel, count, slots, bases), out_sh...  5.66 us
    all_gather x1, blocking collectives, per_device(): row_stats = lax.all_gather(after(stats, (qd_near, qd_other)), 'gx')  4.08 us
    ppermute x2, starting transfers between devices, partner_swap(): lax.ppermute(value, 'gx', [(i, i ^ 1 << level) for i in range(lax.axis_si...  3.79 us
  transfers between devices with their start and end apart: 20, of which 4 were waited for; matrix products, arithmetic and copies ran while one was open for 2% of the time, Pallas kernels for 14%

profile of v2, /device:TPU:1, one launch (start us, length us, event | category | flops | bytes accessed | tf_op | source)
XLA Modules:
  0.0 69.7 jit_solution(8331044751627911675)
XLA Ops:
  0.6 0.1 collective-permute-start
  0.8 0.7 collective-permute-start.1
  1.4 1.2 %collective-permute-done.refs_1_ = bf16[2,128,768]{2,1,0:T(8,128)(2,1)S(1)} collective-permute-done((bf16[2,128,768]{2,1,0:T(8,128)(2,1)}, bf16[2,128,768]{2,1,0:T(8,128)(2,1)S(1)}, u32[]{:S(2)}, u32[]{:S(2)}) %collective-permute-start) | collective-permute-done | bytes 393248 | tf_op jit(solution)/shard_map/kv_X1/ppermute | solution.py:23
  2.6 1.1 %pad_maximum_fusion = bf16[2,128,768]{2,1,0:T(8,128)(2,1)S(1)} fusion(bf16[1,128,768]{2,1,0:T(8,128)(2,1)} %bitcast.26, bf16[1,128,768]{2,1,0:T(8,128)(2,1)} %bitcast.22), kind=kLoop, calls=%fused_computation | loop fusion | flops 196608 | bytes 786432 | tf_op jit(solution)/shard_map/stack | solution.py:226
  3.8 0.2 collective-permute-start.4
  4.0 2.6 %collective-permute-start.7 = (bf16[2,128,768]{2,1,0:T(8,128)(2,1)S(1)}, bf16[2,128,768]{2,1,0:T(8,128)(2,1)S(1)}, u32[]{:S(2)}, u32[]{:S(2)}) collective-permute-start(bf16[2,128,768]{2,1,0:T(8,128)(2,1)S(1)} %bitcast.17), channel_id=1, source_target_pairs={{0,16},{8,24},{16,0},{24,8},{1,17},{9,25},{17,1},{25,9},{2,18},{10... | collective-permute-start | bytes 1179656 | tf_op jit(solution)/shard_map/kv_PT/ppermute | solution.py:27
  6.6 2.8 %collective-permute-start.3 = (bf16[2,128,768]{2,1,0:T(8,128)(2,1)S(1)}, bf16[2,128,768]{2,1,0:T(8,128)(2,1)S(1)}, u32[]{:S(2)}, u32[]{:S(2)}) collective-permute-start(bf16[2,128,768]{2,1,0:T(8,128)(2,1)S(1)} %bitcast.18), channel_id=1, source_target_pairs={{0,1},{1,0},{2,3},{3,2},{4,5},{5,4},{6,7},{7,6},{8,9},{9,8},{10,11... | collective-permute-start | bytes 1179656 | tf_op jit(solution)/shard_map/kv_near/ppermute | solution.py:23
  9.4 0.7 %copy-done.3 = bf16[2,128,768]{2,1,0:T(8,128)(2,1)} copy-done((bf16[2,128,768]{2,1,0:T(8,128)(2,1)}, bf16[2,128,768]{2,1,0:T(8,128)(2,1)S(1)}, u32[]{:S(2)}) %copy-start.3) | copy-done | bytes 393240
  10.1 0.8 %collective-permute-start.5 = (bf16[2,128,768]{2,1,0:T(8,128)(2,1)S(1)}, bf16[2,128,768]{2,1,0:T(8,128)(2,1)S(1)}, u32[]{:S(2)}, u32[]{:S(2)}) collective-permute-start(bf16[2,128,768]{2,1,0:T(8,128)(2,1)S(1)} %collective-permute-done.1.refs_4_), channel_id=1, source_target_pairs={{0,8},{8,0},{16,24},{24,16},{1,9},{9,1},{17,25},{25,17},{2,10},{10... | collective-permute-start | bytes 1179656 | tf_op jit(solution)/shard_map/kvfar_X1/ppermute | solution.py:23
  10.9 2.0 %collective-permute-start.6 = (bf16[2,128,768]{2,1,0:T(8,128)(2,1)S(1)}, bf16[2,128,768]{2,1,0:T(8,128)(2,1)S(1)}, u32[]{:S(2)}, u32[]{:S(2)}) collective-permute-start(bf16[2,128,768]{2,1,0:T(8,128)(2,1)S(1)} %collective-permute-done.1.refs_4_), channel_id=1, source_target_pairs={{8,16},{16,8},{9,17},{17,9},{10,18},{18,10},{11,19},{19,11},{12,20... | collective-permute-start | bytes 1179656 | tf_op jit(solution)/shard_map/kvfar_X2/ppermute | solution.py:23
  12.9 3.0 %collective-permute-done.7.refs_3_ = bf16[2,128,768]{2,1,0:T(8,128)(2,1)S(1)} collective-permute-done((bf16[2,128,768]{2,1,0:T(8,128)(2,1)S(1)}, bf16[2,128,768]{2,1,0:T(8,128)(2,1)S(1)}, u32[]{:S(2)}, u32[]{:S(2)}) %collective-permute-start.7) | collective-permute-done | bytes 393248 | tf_op jit(solution)/shard_map/kv_PT/ppermute | solution.py:27
  15.9 0.7 %collective-permute-start.8 = (bf16[2,128,768]{2,1,0:T(8,128)(2,1)S(1)}, bf16[2,128,768]{2,1,0:T(8,128)(2,1)S(1)}, u32[]{:S(2)}, u32[]{:S(2)}) collective-permute-start(bf16[2,128,768]{2,1,0:T(8,128)(2,1)S(1)} %collective-permute-done.7.refs_3_), channel_id=1, source_target_pairs={{0,8},{8,0},{16,24},{24,16},{1,9},{9,1},{17,25},{25,17},{2,10},{10... | collective-permute-start | bytes 1179656 | tf_op jit(solution)/shard_map/kv_PT_X1/ppermute | solution.py:23
  16.6 0.1 stack.37
  16.7 0.1 stack.34
  16.8 0.7 collective-permute-start.2
  17.5 6.2 %collective-permute-done.3.refs_7_ = bf16[2,128,768]{2,1,0:T(8,128)(2,1)S(1)} collective-permute-done((bf16[2,128,768]{2,1,0:T(8,128)(2,1)S(1)}, bf16[2,128,768]{2,1,0:T(8,128)(2,1)S(1)}, u32[]{:S(2)}, u32[]{:S(2)}) %collective-permute-start.3) | collective-permute-done | bytes 393248 | tf_op jit(solution)/shard_map/kv_near/ppermute | solution.py:23
  23.7 1.2 %collective-permute-start.13 = (bf16[2,128,768]{2,1,0:T(8,128)(2,1)}, bf16[2,128,768]{2,1,0:T(8,128)(2,1)S(1)}, u32[]{:S(2)}, u32[]{:S(2)}) collective-permute-start(bf16[2,128,768]{2,1,0:T(8,128)(2,1)} %copy-done.5), channel_id=1, source_target_pairs={{0,16},{8,24},{16,0},{24,8},{1,17},{9,25},{17,1},{25,9},{2,18},{10... | collective-permute-start | bytes 1179656 | tf_op jit(solution)/shard_map/qd_PT/ppermute | solution.py:27
  24.9 0.8 %collective-permute-start.9 = (bf16[2,128,768]{2,1,0:T(8,128)(2,1)S(1)}, bf16[2,128,768]{2,1,0:T(8,128)(2,1)S(1)}, u32[]{:S(2)}, u32[]{:S(2)}) collective-permute-start(bf16[2,128,768]{2,1,0:T(8,128)(2,1)S(1)} %collective-permute-done.3.refs_7_), channel_id=1, source_target_pairs={{0,8},{8,0},{16,24},{24,16},{1,9},{9,1},{17,25},{25,17},{2,10},{10... | collective-permute-start | bytes 1179656 | tf_op jit(solution)/shard_map/kvnear_X1/ppermute | solution.py:23
  25.8 2.3 %collective-permute-start.12 = (bf16[2,128,768]{2,1,0:T(8,128)(2,1)}, bf16[2,128,768]{2,1,0:T(8,128)(2,1)S(1)}, u32[]{:S(2)}, u32[]{:S(2)}) collective-permute-start(bf16[2,128,768]{2,1,0:T(8,128)(2,1)} %copy-done.5), channel_id=1, source_target_pairs={{0,1},{1,0},{2,3},{3,2},{4,5},{5,4},{6,7},{7,6},{8,9},{9,8},{10,11... | collective-permute-start | bytes 1179656 | tf_op jit(solution)/shard_map/qd_near/ppermute | solution.py:23
  28.0 3.2 %collective-permute-start.11 = (bf16[2,128,768]{2,1,0:T(8,128)(2,1)S(1)}, bf16[2,128,768]{2,1,0:T(8,128)(2,1)S(1)}, u32[]{:S(2)}, u32[]{:S(2)}) collective-permute-start(bf16[2,128,768]{2,1,0:T(8,128)(2,1)S(1)} %collective-permute-done.3.refs_7_), channel_id=1, source_target_pairs={{8,16},{16,8},{9,17},{17,9},{10,18},{18,10},{11,19},{19,11},{12,20... | collective-permute-start | bytes 1179656 | tf_op jit(solution)/shard_map/kvnear_X2/ppermute | solution.py:23
  31.3 2.8 %collective-permute-done.13.refs_2_ = bf16[2,128,768]{2,1,0:T(8,128)(2,1)S(1)} collective-permute-done((bf16[2,128,768]{2,1,0:T(8,128)(2,1)}, bf16[2,128,768]{2,1,0:T(8,128)(2,1)S(1)}, u32[]{:S(2)}, u32[]{:S(2)}) %collective-permute-start.13) | collective-permute-done | bytes 393248 | tf_op jit(solution)/shard_map/qd_PT/ppermute | solution.py:27
  34.1 1.4 %collective-permute-start.14 = (bf16[2,128,768]{2,1,0:T(8,128)(2,1)S(1)}, bf16[2,128,768]{2,1,0:T(8,128)(2,1)S(1)}, u32[]{:S(2)}, u32[]{:S(2)}) collective-permute-start(bf16[2,128,768]{2,1,0:T(8,128)(2,1)S(1)} %collective-permute-done.13.refs_2_), channel_id=1, source_target_pairs={{0,8},{8,0},{16,24},{24,16},{1,9},{9,1},{17,25},{25,17},{2,10},{10... | collective-permute-start | bytes 1179656 | tf_op jit(solution)/shard_map/qd_PT_X1/ppermute | solution.py:23
  35.6 0.2 select_reduce_fusion
  35.8 4.3 %collective-permute-start.15 = (bf16[2,128,768]{2,1,0:T(8,128)(2,1)S(1)}, bf16[2,128,768]{2,1,0:T(8,128)(2,1)S(1)}, u32[]{:S(2)}, u32[]{:S(2)}) collective-permute-start(bf16[2,128,768]{2,1,0:T(8,128)(2,1)S(1)} %collective-permute-done.2.refs_3_), channel_id=1, source_target_pairs={{8,16},{16,8},{9,17},{17,9},{10,18},{18,10},{11,19},{19,11},{12,20... | collective-permute-start | bytes 1179656 | tf_op jit(solution)/shard_map/qdfar_X2/ppermute | solution.py:23
  40.1 5.3 %shard_map.67 = (bf16[128,768]{1,0:T(8,128)(2,1)}, f32[128,128]{1,0:T(8,128)S(1)}, f32[32,128]{1,0:T(8,128)S(1)}) custom-call(f32[10]{0:T(128)S(1)} %or_select_fusion.bias_ref, bf16[128,768]{1,0:T(8,128)(2,1)S(1)} %bitcast.23, bf16[128,768]{1,0:T(8,128)(2,1)S(1)} %bitcast.27, f32[8,128]{1,0:T(8,128)S(1)} %broadcast_in_dim.57.flags_ref, ...), custom_call_target="tpu_custom_call" | custom-call | flops 128 | bytes 128 | tf_op jit(solution)/shard_map/pallas_call | solution.py:272
  45.5 4.1 %all-gather = f32[128,128]{1,0:T(8,128)S(1)} all-gather(f32[32,128]{1,0:T(8,128)S(1)} %get-tuple-element.30), channel_id=2, replica_groups=mesh['gx'=4,'gy'=8] {'gx'}, dimensions={0}, use_global_device_ids=true | all-gather | bytes 81920 | tf_op jit(solution)/shard_map/stats_row/all_gather | solution.py:290
  49.6 0.3 collective-permute-start.16
  49.9 3.7 %collective-permute-start.17 = (bf16[2,128,768]{2,1,0:T(8,128)(2,1)S(1)}, bf16[2,128,768]{2,1,0:T(8,128)(2,1)S(1)}, u32[]{:S(2)}, u32[]{:S(2)}) collective-permute-start(bf16[2,128,768]{2,1,0:T(8,128)(2,1)S(1)} %collective-permute-done.12.refs_6_), channel_id=1, source_target_pairs={{8,16},{16,8},{9,17},{17,9},{10,18},{18,10},{11,19},{19,11},{12,20... | collective-permute-start | bytes 1179656 | tf_op jit(solution)/shard_map/qdnear_X2/ppermute | solution.py:23
  53.7 0.8 %collective-permute-start.18 = (f32[4,32,128]{2,1,0:T(8,128)S(1)}, f32[4,32,128]{2,1,0:T(8,128)S(1)}, u32[]{:S(2)}, u32[]{:S(2)}) collective-permute-start(f32[4,32,128]{2,1,0:T(8,128)S(1)} %bitcast.30), channel_id=1, source_target_pairs={{1,2},{2,1},{3,4},{4,3},{5,6},{6,5},{9,10},{10,9},{11,12},{12,11},... | collective-permute-start | bytes 196616 | tf_op jit(solution)/shard_map/stats_far/ppermute | solution.py:23
  54.5 4.7 %collective-permute-start.19 = (f32[4,32,128]{2,1,0:T(8,128)S(1)}, f32[4,32,128]{2,1,0:T(8,128)S(1)}, u32[]{:S(2)}, u32[]{:S(2)}) collective-permute-start(f32[4,32,128]{2,1,0:T(8,128)S(1)} %bitcast.31), channel_id=1, source_target_pairs={{0,1},{1,0},{2,3},{3,2},{4,5},{5,4},{6,7},{7,6},{8,9},{9,8},{10,11... | collective-permute-start | bytes 196616 | tf_op jit(solution)/shard_map/stats_near/ppermute | solution.py:23
  59.3 4.7 %shard_map.68 = bf16[128,768]{1,0:T(8,128)(2,1)} custom-call(f32[10]{0:T(128)S(1)} %or_select_fusion.bias_ref, bf16[128,768]{1,0:T(8,128)(2,1)S(1)} %bitcast.24, bf16[128,768]{1,0:T(8,128)(2,1)S(1)} %bitcast.28, f32[128,128]{1,0:T(8,128)S(1)} %get-tuple-element.31.columns_ref, bf16[2,128,768]{2,1,0:T(8,128)(2,1)S(1)} %bitcast.20, ...), custom_call_target="tpu_custom_call" | custom-call | flops 128 | bytes 128 | tf_op jit(solution)/shard_map/pallas_call | solution.py:272
  64.0 5.7 %shard_map.69 = bf16[2,128,768]{2,1,0:T(8,128)(2,1)} custom-call(s32[10]{0:T(128)S(1)} %broadcast_clamp_fusion.index_ref, f32[10,128]{1,0:T(8,128)S(1)} %fusion.choose_ref, bf16[2,128,768]{2,1,0:T(8,128)(2,1)S(1)} %bitcast.21, bf16[128,768]{1,0:T(8,128)(2,1)S(1)} %bitcast.25, bf16[128,768]{1,0:T(8,128)(2,1)S(1)} %bitcast.29, ...), custom_call_target="tpu_custom_call" | custom-call | flops 128 | bytes 128 | tf_op jit(solution)/shard_map/pallas_call | solution.py:303
  (39 shorter events, 0.2 us)
Async XLA Ops:
  0.6 2.0 %collective-permute-start = (bf16[2,128,768]{2,1,0:T(8,128)(2,1)}, bf16[2,128,768]{2,1,0:T(8,128)(2,1)S(1)}, u32[]{:S(2)}, u32[]{:S(2)}) collective-permute-start(bf16[2,128,768]{2,1,0:T(8,128)(2,1)} %bitcast.15), channel_id=1, source_target_pairs={{0,8},{8,0},{16,24},{24,16},{1,9},{9,1},{17,25},{25,17},{2,10},{10... | collective-permute-start | bytes 1179656 | tf_op jit(solution)/shard_map/kv_X1/ppermute | solution.py:23
  0.8 8.6 %collective-permute-start.1 = (bf16[2,128,768]{2,1,0:T(8,128)(2,1)}, bf16[2,128,768]{2,1,0:T(8,128)(2,1)S(1)}, u32[]{:S(2)}, u32[]{:S(2)}) collective-permute-start(bf16[2,128,768]{2,1,0:T(8,128)(2,1)} %bitcast.16), channel_id=1, source_target_pairs={{1,2},{2,1},{3,4},{4,3},{5,6},{6,5},{9,10},{10,9},{11,12},{12,11},... | collective-permute-start | bytes 1179656 | tf_op jit(solution)/shard_map/kv_far/ppermute | solution.py:23
  2.6 1.4 %copy-start = (bf16[1,1,2,128,768]{4,3,2,1,0:T(8,128)(2,1)S(1)}, bf16[1,1,2,128,768]{4,3,2,1,0:T(8,128)(2,1)}, u32[]{:S(2)}) copy-start(bf16[1,1,2,128,768]{4,3,2,1,0:T(8,128)(2,1)} %param.5) | copy-start | bytes 1179652
  2.6 37.5 %copy-start.1 = (bf16[1,1,128,768]{3,2,1,0:T(8,128)(2,1)S(1)}, bf16[1,1,128,768]{3,2,1,0:T(8,128)(2,1)}, u32[]{:S(2)}) copy-start(bf16[1,1,128,768]{3,2,1,0:T(8,128)(2,1)} %param.4) | copy-start | bytes 589828
  2.6 37.5 %copy-start.2 = (bf16[1,1,128,768]{3,2,1,0:T(8,128)(2,1)S(1)}, bf16[1,1,128,768]{3,2,1,0:T(8,128)(2,1)}, u32[]{:S(2)}) copy-start(bf16[1,1,128,768]{3,2,1,0:T(8,128)(2,1)} %param.6) | copy-start | bytes 589828
  3.8 12.2 %copy-start.5 = (bf16[2,128,768]{2,1,0:T(8,128)(2,1)}, bf16[2,128,768]{2,1,0:T(8,128)(2,1)S(1)}, u32[]{:S(2)}) copy-start(bf16[2,128,768]{2,1,0:T(8,128)(2,1)S(1)} %pad_maximum_fusion) | copy-start | bytes 1179652
  3.8 5.6 %collective-permute-start.4 = (bf16[2,128,768]{2,1,0:T(8,128)(2,1)S(1)}, bf16[2,128,768]{2,1,0:T(8,128)(2,1)S(1)}, u32[]{:S(2)}, u32[]{:S(2)}) collective-permute-start(bf16[2,128,768]{2,1,0:T(8,128)(2,1)S(1)} %pad_maximum_fusion), channel_id=1, source_target_pairs={{0,8},{8,0},{16,24},{24,16},{1,9},{9,1},{17,25},{25,17},{2,10},{10... | collective-permute-start | bytes 1179656 | tf_op jit(solution)/shard_map/qd_X1/ppermute | solution.py:23
  4.0 11.9 %collective-permute-start.7 = (bf16[2,128,768]{2,1,0:T(8,128)(2,1)S(1)}, bf16[2,128,768]{2,1,0:T(8,128)(2,1)S(1)}, u32[]{:S(2)}, u32[]{:S(2)}) collective-permute-start(bf16[2,128,768]{2,1,0:T(8,128)(2,1)S(1)} %bitcast.17), channel_id=1, source_target_pairs={{0,16},{8,24},{16,0},{24,8},{1,17},{9,25},{17,1},{25,9},{2,18},{10... | collective-permute-start | bytes 1179656 | tf_op jit(solution)/shard_map/kv_PT/ppermute | solution.py:27
  6.6 17.1 %collective-permute-start.3 = (bf16[2,128,768]{2,1,0:T(8,128)(2,1)S(1)}, bf16[2,128,768]{2,1,0:T(8,128)(2,1)S(1)}, u32[]{:S(2)}, u32[]{:S(2)}) collective-permute-start(bf16[2,128,768]{2,1,0:T(8,128)(2,1)S(1)} %bitcast.18), channel_id=1, source_target_pairs={{0,1},{1,0},{2,3},{3,2},{4,5},{5,4},{6,7},{7,6},{8,9},{9,8},{10,11... | collective-permute-start | bytes 1179656 | tf_op jit(solution)/shard_map/kv_near/ppermute | solution.py:23
  9.4 0.7 %copy-start.3 = (bf16[2,128,768]{2,1,0:T(8,128)(2,1)}, bf16[2,128,768]{2,1,0:T(8,128)(2,1)S(1)}, u32[]{:S(2)}) copy-start(bf16[2,128,768]{2,1,0:T(8,128)(2,1)S(1)} %collective-permute-done.4.refs_0_) | copy-start | bytes 1179652
  10.1 14.8 %collective-permute-start.5 = (bf16[2,128,768]{2,1,0:T(8,128)(2,1)S(1)}, bf16[2,128,768]{2,1,0:T(8,128)(2,1)S(1)}, u32[]{:S(2)}, u32[]{:S(2)}) collective-permute-start(bf16[2,128,768]{2,1,0:T(8,128)(2,1)S(1)} %collective-permute-done.1.refs_4_), channel_id=1, source_target_pairs={{0,8},{8,0},{16,24},{24,16},{1,9},{9,1},{17,25},{25,17},{2,10},{10... | collective-permute-start | bytes 1179656 | tf_op jit(solution)/shard_map/kvfar_X1/ppermute | solution.py:23
  10.9 14.0 %collective-permute-start.6 = (bf16[2,128,768]{2,1,0:T(8,128)(2,1)S(1)}, bf16[2,128,768]{2,1,0:T(8,128)(2,1)S(1)}, u32[]{:S(2)}, u32[]{:S(2)}) collective-permute-start(bf16[2,128,768]{2,1,0:T(8,128)(2,1)S(1)} %collective-permute-done.1.refs_4_), channel_id=1, source_target_pairs={{8,16},{16,8},{9,17},{17,9},{10,18},{18,10},{11,19},{19,11},{12,20... | collective-permute-start | bytes 1179656 | tf_op jit(solution)/shard_map/kvfar_X2/ppermute | solution.py:23
  15.9 9.0 %collective-permute-start.8 = (bf16[2,128,768]{2,1,0:T(8,128)(2,1)S(1)}, bf16[2,128,768]{2,1,0:T(8,128)(2,1)S(1)}, u32[]{:S(2)}, u32[]{:S(2)}) collective-permute-start(bf16[2,128,768]{2,1,0:T(8,128)(2,1)S(1)} %collective-permute-done.7.refs_3_), channel_id=1, source_target_pairs={{0,8},{8,0},{16,24},{24,16},{1,9},{9,1},{17,25},{25,17},{2,10},{10... | collective-permute-start | bytes 1179656 | tf_op jit(solution)/shard_map/kv_PT_X1/ppermute | solution.py:23
  16.7 9.0 %copy-start.6 = (s32[1,1,9]{2,1,0:T(1,128)S(1)}, s32[1,1,9]{2,1,0:T(1,128)}, u32[]{:S(2)}) copy-start(s32[1,1,9]{2,1,0:T(1,128)} %param.7) | copy-start | bytes 112
  16.8 18.7 %collective-permute-start.2 = (bf16[2,128,768]{2,1,0:T(8,128)(2,1)}, bf16[2,128,768]{2,1,0:T(8,128)(2,1)S(1)}, u32[]{:S(2)}, u32[]{:S(2)}) collective-permute-start(bf16[2,128,768]{2,1,0:T(8,128)(2,1)} %copy-done.5), channel_id=1, source_target_pairs={{1,2},{2,1},{3,4},{4,3},{5,6},{6,5},{9,10},{10,9},{11,12},{12,11},... | collective-permute-start | bytes 1179656 | tf_op jit(solution)/shard_map/qd_far/ppermute | solution.py:23
  23.7 10.4 %collective-permute-start.13 = (bf16[2,128,768]{2,1,0:T(8,128)(2,1)}, bf16[2,128,768]{2,1,0:T(8,128)(2,1)S(1)}, u32[]{:S(2)}, u32[]{:S(2)}) collective-permute-start(bf16[2,128,768]{2,1,0:T(8,128)(2,1)} %copy-done.5), channel_id=1, source_target_pairs={{0,16},{8,24},{16,0},{24,8},{1,17},{9,25},{17,1},{25,9},{2,18},{10... | collective-permute-start | bytes 1179656 | tf_op jit(solution)/shard_map/qd_PT/ppermute | solution.py:27
  24.9 10.6 %collective-permute-start.9 = (bf16[2,128,768]{2,1,0:T(8,128)(2,1)S(1)}, bf16[2,128,768]{2,1,0:T(8,128)(2,1)S(1)}, u32[]{:S(2)}, u32[]{:S(2)}) collective-permute-start(bf16[2,128,768]{2,1,0:T(8,128)(2,1)S(1)} %collective-permute-done.3.refs_7_), channel_id=1, source_target_pairs={{0,8},{8,0},{16,24},{24,16},{1,9},{9,1},{17,25},{25,17},{2,10},{10... | collective-permute-start | bytes 1179656 | tf_op jit(solution)/shard_map/kvnear_X1/ppermute | solution.py:23
  25.8 19.7 %collective-permute-start.12 = (bf16[2,128,768]{2,1,0:T(8,128)(2,1)}, bf16[2,128,768]{2,1,0:T(8,128)(2,1)S(1)}, u32[]{:S(2)}, u32[]{:S(2)}) collective-permute-start(bf16[2,128,768]{2,1,0:T(8,128)(2,1)} %copy-done.5), channel_id=1, source_target_pairs={{0,1},{1,0},{2,3},{3,2},{4,5},{5,4},{6,7},{7,6},{8,9},{9,8},{10,11... | collective-permute-start | bytes 1179656 | tf_op jit(solution)/shard_map/qd_near/ppermute | solution.py:23
  28.0 12.1 %collective-permute-start.11 = (bf16[2,128,768]{2,1,0:T(8,128)(2,1)S(1)}, bf16[2,128,768]{2,1,0:T(8,128)(2,1)S(1)}, u32[]{:S(2)}, u32[]{:S(2)}) collective-permute-start(bf16[2,128,768]{2,1,0:T(8,128)(2,1)S(1)} %collective-permute-done.3.refs_7_), channel_id=1, source_target_pairs={{8,16},{16,8},{9,17},{17,9},{10,18},{18,10},{11,19},{19,11},{12,20... | collective-permute-start | bytes 1179656 | tf_op jit(solution)/shard_map/kvnear_X2/ppermute | solution.py:23
  34.1 11.4 %collective-permute-start.14 = (bf16[2,128,768]{2,1,0:T(8,128)(2,1)S(1)}, bf16[2,128,768]{2,1,0:T(8,128)(2,1)S(1)}, u32[]{:S(2)}, u32[]{:S(2)}) collective-permute-start(bf16[2,128,768]{2,1,0:T(8,128)(2,1)S(1)} %collective-permute-done.13.refs_2_), channel_id=1, source_target_pairs={{0,8},{8,0},{16,24},{24,16},{1,9},{9,1},{17,25},{25,17},{2,10},{10... | collective-permute-start | bytes 1179656 | tf_op jit(solution)/shard_map/qd_PT_X1/ppermute | solution.py:23
  35.5 4.6 %collective-permute-start.10 = (bf16[2,128,768]{2,1,0:T(8,128)(2,1)S(1)}, bf16[2,128,768]{2,1,0:T(8,128)(2,1)S(1)}, u32[]{:S(2)}, u32[]{:S(2)}) collective-permute-start(bf16[2,128,768]{2,1,0:T(8,128)(2,1)S(1)} %collective-permute-done.2.refs_3_), channel_id=1, source_target_pairs={{0,8},{8,0},{16,24},{24,16},{1,9},{9,1},{17,25},{25,17},{2,10},{10... | collective-permute-start | bytes 1179656 | tf_op jit(solution)/shard_map/qdfar_X1/ppermute | solution.py:23
  35.8 28.2 %collective-permute-start.15 = (bf16[2,128,768]{2,1,0:T(8,128)(2,1)S(1)}, bf16[2,128,768]{2,1,0:T(8,128)(2,1)S(1)}, u32[]{:S(2)}, u32[]{:S(2)}) collective-permute-start(bf16[2,128,768]{2,1,0:T(8,128)(2,1)S(1)} %collective-permute-done.2.refs_3_), channel_id=1, source_target_pairs={{8,16},{16,8},{9,17},{17,9},{10,18},{18,10},{11,19},{19,11},{12,20... | collective-permute-start | bytes 1179656 | tf_op jit(solution)/shard_map/qdfar_X2/ppermute | solution.py:23
  49.6 14.4 %collective-permute-start.16 = (bf16[2,128,768]{2,1,0:T(8,128)(2,1)S(1)}, bf16[2,128,768]{2,1,0:T(8,128)(2,1)S(1)}, u32[]{:S(2)}, u32[]{:S(2)}) collective-permute-start(bf16[2,128,768]{2,1,0:T(8,128)(2,1)S(1)} %collective-permute-done.12.refs_6_), channel_id=1, source_target_pairs={{0,8},{8,0},{16,24},{24,16},{1,9},{9,1},{17,25},{25,17},{2,10},{10... | collective-permute-start | bytes 1179656 | tf_op jit(solution)/shard_map/qdnear_X1/ppermute | solution.py:23
  49.9 14.1 %collective-permute-start.17 = (bf16[2,128,768]{2,1,0:T(8,128)(2,1)S(1)}, bf16[2,128,768]{2,1,0:T(8,128)(2,1)S(1)}, u32[]{:S(2)}, u32[]{:S(2)}) collective-permute-start(bf16[2,128,768]{2,1,0:T(8,128)(2,1)S(1)} %collective-permute-done.12.refs_6_), channel_id=1, source_target_pairs={{8,16},{16,8},{9,17},{17,9},{10,18},{18,10},{11,19},{19,11},{12,20... | collective-permute-start | bytes 1179656 | tf_op jit(solution)/shard_map/qdnear_X2/ppermute | solution.py:23
  53.7 10.3 %collective-permute-start.18 = (f32[4,32,128]{2,1,0:T(8,128)S(1)}, f32[4,32,128]{2,1,0:T(8,128)S(1)}, u32[]{:S(2)}, u32[]{:S(2)}) collective-permute-start(f32[4,32,128]{2,1,0:T(8,128)S(1)} %bitcast.30), channel_id=1, source_target_pairs={{1,2},{2,1},{3,4},{4,3},{5,6},{6,5},{9,10},{10,9},{11,12},{12,11},... | collective-permute-start | bytes 196616 | tf_op jit(solution)/shard_map/stats_far/ppermute | solution.py:23
  54.5 9.5 %collective-permute-start.19 = (f32[4,32,128]{2,1,0:T(8,128)S(1)}, f32[4,32,128]{2,1,0:T(8,128)S(1)}, u32[]{:S(2)}, u32[]{:S(2)}) collective-permute-start(f32[4,32,128]{2,1,0:T(8,128)S(1)} %bitcast.31), channel_id=1, source_target_pairs={{0,1},{1,0},{2,3},{3,2},{4,5},{5,4},{6,7},{7,6},{8,9},{9,8},{10,11... | collective-permute-start | bytes 196616 | tf_op jit(solution)/shard_map/stats_near/ppermute | solution.py:23
  59.3 4.7 %copy-start.4 = (bf16[2,128,768]{2,1,0:T(8,128)(2,1)S(1)}, bf16[2,128,768]{2,1,0:T(8,128)(2,1)}, u32[]{:S(2)}) copy-start(bf16[2,128,768]{2,1,0:T(8,128)(2,1)} %copy-done.3) | copy-start | bytes 1179652

commit v3 on v2

--- a/solution.py
+++ b/solution.py
@@ -74,8 +74,12 @@
         scores = jnp.concatenate(scores, axis=1)
         largest = jnp.max(scores, axis=1, keepdims=True) * FOLD
         raised = jnp.exp2(scores * FOLD - largest)
-        totals = jnp.sum(raised, axis=1, keepdims=True)
-        sums = jnp.dot(raised.astype(jnp.bfloat16), values, preferred_element_type=jnp.float32)
+        sums = jnp.dot(
+            raised.astype(jnp.bfloat16),
+            jnp.concatenate([values, jnp.ones_like(values)], axis=1),
+            preferred_element_type=jnp.float32,
+        )
+        sums, totals = sums[:, :LANES], sums[:, LANES:]
         attended = join_heads(sums * (1.0 / totals)).astype(jnp.bfloat16)
         att_ref[:, cols] = attended
         product = do_ref[:, cols].astype(jnp.float32) * attended.astype(jnp.float32)
@@ -86,7 +90,7 @@
             ],
             axis=0,
         )
-        columns = per_lane(largest + jnp.log2(totals), lane, 2 * pair, columns)
+        columns = per_lane(largest + jnp.log2(totals[:, :1]), lane, 2 * pair, columns)
         columns = per_lane(delta, lane, heads + 2 * pair, columns)
     columns_ref[...] = columns
     stats_ref[: 2 * heads] = columns.T[: 2 * heads]
@@ -280,20 +284,21 @@
 
     wide = jax.ShapeDtypeStruct((rows, width), jnp.bfloat16)
     table = jax.ShapeDtypeStruct((rows, LANES), jnp.float32)
+    near_q, near_do = on_chip(own_q), on_chip(own_do)
     bias = after(bias, qd_far1)
     attended, columns_of, stats = call(
         functools.partial(attend_kernel, count),
-        (bias, own_q, own_do, flags, *kv_blocks),
+        (bias, near_q, near_do, on_chip(flags), *kv_blocks),
         (wide, table, jax.ShapeDtypeStruct((2 * heads + 8, LANES), jnp.float32)),
     )
     with jax.named_scope("stats_row"):
-        row_stats = lax.all_gather(after(stats, (qd_near, qd_other)), "gx")
+        row_stats = lax.all_gather(after(stats, qd_other), "gx")
     ready = after(qd_near, row_stats)
     qd_near1, qd_near2 = core_pair(ready, "qdnear"), link_pair(ready, "qdnear")
     far_stats, near_stats = far(row_stats, "stats"), near(row_stats, "stats")
     query_grad = call(
         functools.partial(query_kernel, count),
-        (bias, own_q, own_do, after(columns_of, row_stats), *kv_blocks),
+        (bias, near_q, near_do, on_chip(after(columns_of, row_stats)), *kv_blocks),
         wide,
     )
     qd_blocks = [qd_pair, qd_other] + qd_partners
@@ -307,7 +312,15 @@
         out_specs=VMEM,
         compiler_params=PARAMS,
         cost_estimate=COST,
-    )(index, choose, own_kv, own_q, own_do, *qd_blocks, row_stats, far_stats, near_stats)
+    )(
+        index,
+        on_chip(choose),
+        kv_blocks[0],
+        near_q,
+        near_do,
+        *qd_blocks,
+        *[on_chip(v) for v in (row_stats, far_stats, near_stats)],
+    )
     return attended[None, None], query_grad[None, None], key_value_grad[None, None]
 
 

time: 69.9 us -> 68.9 us (0.986)
  Pallas kernels: 15.7 us -> 14.7 us
    pallas_call x2, Pallas kernels: 10 us -> 9.04 us  [call(): pl.pallas_call(kernel, out_shape=outputs, in_specs=[SMEM] + [VMEM] * (len...]
  transfers between devices with their start and end apart: 20 -> 20, of which waited for: 4 -> 4; matrix products, arithmetic and copies ran while one was open for 2% -> 2% of each run, Pallas kernels for 14% -> 13%
where the time goes in v3:
time: 68.9 us; the launch traced here: 68.7 us
  starting transfers between devices  33.5 us (49%)
  Pallas kernels  14.7 us (21%)
  waiting for transfers between devices  13.2 us (19%)
  blocking collectives  4.08 us (6%)
  other arithmetic  1.42 us (2%)
  local copies, waits for them, and re-layouts  0.94 us (1%)
  between operations  0.8 us (1%)
    ppermute x18, starting transfers between devices, pair_swap(): return lax.ppermute(value, axis, pairs)  29.7 us
    pallas_call x2, Pallas kernels, call(): pl.pallas_call(kernel, out_shape=outputs, in_specs=[SMEM] + [VMEM] * (len...  9.04 us
    ppermute x18, waiting for transfers between devices, pair_swap(): return lax.ppermute(value, axis, pairs)  7.43 us
    ppermute x2, waiting for transfers between devices, partner_swap(): lax.ppermute(value, 'gx', [(i, i ^ 1 << level) for i in range(lax.axis_si...  5.81 us
    pallas_call x1, Pallas kernels, per_device(): pl.pallas_call(functools.partial(key_kernel, count, slots, bases), out_sh...  5.66 us
    all_gather x1, blocking collectives, per_device(): row_stats = lax.all_gather(after(stats, qd_other), 'gx')  4.08 us
    ppermute x2, starting transfers between devices, partner_swap(): lax.ppermute(value, 'gx', [(i, i ^ 1 << level) for i in range(lax.axis_si...  3.79 us
  transfers between devices with their start and end apart: 20, of which 4 were waited for; matrix products, arithmetic and copies ran while one was open for 2% of the time, Pallas kernels for 13%

profile of v3, /device:TPU:1, one launch (start us, length us, event | category | flops | bytes accessed | tf_op | source)
XLA Modules:
  0.0 68.7 jit_solution(5663060033359833406)
XLA Ops:
  0.6 0.1 collective-permute-start
  0.8 0.7 collective-permute-start.1
  1.4 1.2 %collective-permute-done.refs_1_ = bf16[2,128,768]{2,1,0:T(8,128)(2,1)S(1)} collective-permute-done((bf16[2,128,768]{2,1,0:T(8,128)(2,1)}, bf16[2,128,768]{2,1,0:T(8,128)(2,1)S(1)}, u32[]{:S(2)}, u32[]{:S(2)}) %collective-permute-start) | collective-permute-done | bytes 393248 | tf_op jit(solution)/shard_map/kv_X1/ppermute | solution.py:23
  2.6 1.1 %pad_maximum_fusion = bf16[2,128,768]{2,1,0:T(8,128)(2,1)S(1)} fusion(bf16[1,128,768]{2,1,0:T(8,128)(2,1)} %bitcast.26, bf16[1,128,768]{2,1,0:T(8,128)(2,1)} %bitcast.22), kind=kLoop, calls=%fused_computation | loop fusion | flops 196608 | bytes 786432 | tf_op jit(solution)/shard_map/stack | solution.py:230
  3.8 0.2 collective-permute-start.4
  4.0 2.6 %collective-permute-start.7 = (bf16[2,128,768]{2,1,0:T(8,128)(2,1)S(1)}, bf16[2,128,768]{2,1,0:T(8,128)(2,1)S(1)}, u32[]{:S(2)}, u32[]{:S(2)}) collective-permute-start(bf16[2,128,768]{2,1,0:T(8,128)(2,1)S(1)} %bitcast.17), channel_id=1, source_target_pairs={{0,16},{8,24},{16,0},{24,8},{1,17},{9,25},{17,1},{25,9},{2,18},{10... | collective-permute-start | bytes 1179656 | tf_op jit(solution)/shard_map/kv_PT/ppermute | solution.py:27
  6.6 2.8 %collective-permute-start.3 = (bf16[2,128,768]{2,1,0:T(8,128)(2,1)S(1)}, bf16[2,128,768]{2,1,0:T(8,128)(2,1)S(1)}, u32[]{:S(2)}, u32[]{:S(2)}) collective-permute-start(bf16[2,128,768]{2,1,0:T(8,128)(2,1)S(1)} %bitcast.18), channel_id=1, source_target_pairs={{0,1},{1,0},{2,3},{3,2},{4,5},{5,4},{6,7},{7,6},{8,9},{9,8},{10,11... | collective-permute-start | bytes 1179656 | tf_op jit(solution)/shard_map/kv_near/ppermute | solution.py:23
  9.4 0.7 %copy-done.3 = bf16[2,128,768]{2,1,0:T(8,128)(2,1)} copy-done((bf16[2,128,768]{2,1,0:T(8,128)(2,1)}, bf16[2,128,768]{2,1,0:T(8,128)(2,1)S(1)}, u32[]{:S(2)}) %copy-start.3) | copy-done | bytes 393240
  10.1 0.8 %collective-permute-start.5 = (bf16[2,128,768]{2,1,0:T(8,128)(2,1)S(1)}, bf16[2,128,768]{2,1,0:T(8,128)(2,1)S(1)}, u32[]{:S(2)}, u32[]{:S(2)}) collective-permute-start(bf16[2,128,768]{2,1,0:T(8,128)(2,1)S(1)} %collective-permute-done.1.refs_4_), channel_id=1, source_target_pairs={{0,8},{8,0},{16,24},{24,16},{1,9},{9,1},{17,25},{25,17},{2,10},{10... | collective-permute-start | bytes 1179656 | tf_op jit(solution)/shard_map/kvfar_X1/ppermute | solution.py:23
  10.9 2.0 %collective-permute-start.6 = (bf16[2,128,768]{2,1,0:T(8,128)(2,1)S(1)}, bf16[2,128,768]{2,1,0:T(8,128)(2,1)S(1)}, u32[]{:S(2)}, u32[]{:S(2)}) collective-permute-start(bf16[2,128,768]{2,1,0:T(8,128)(2,1)S(1)} %collective-permute-done.1.refs_4_), channel_id=1, source_target_pairs={{8,16},{16,8},{9,17},{17,9},{10,18},{18,10},{11,19},{19,11},{12,20... | collective-permute-start | bytes 1179656 | tf_op jit(solution)/shard_map/kvfar_X2/ppermute | solution.py:23
  12.9 3.0 %collective-permute-done.7.refs_3_ = bf16[2,128,768]{2,1,0:T(8,128)(2,1)S(1)} collective-permute-done((bf16[2,128,768]{2,1,0:T(8,128)(2,1)S(1)}, bf16[2,128,768]{2,1,0:T(8,128)(2,1)S(1)}, u32[]{:S(2)}, u32[]{:S(2)}) %collective-permute-start.7) | collective-permute-done | bytes 393248 | tf_op jit(solution)/shard_map/kv_PT/ppermute | solution.py:27
  15.9 0.7 %collective-permute-start.8 = (bf16[2,128,768]{2,1,0:T(8,128)(2,1)S(1)}, bf16[2,128,768]{2,1,0:T(8,128)(2,1)S(1)}, u32[]{:S(2)}, u32[]{:S(2)}) collective-permute-start(bf16[2,128,768]{2,1,0:T(8,128)(2,1)S(1)} %collective-permute-done.7.refs_3_), channel_id=1, source_target_pairs={{0,8},{8,0},{16,24},{24,16},{1,9},{9,1},{17,25},{25,17},{2,10},{10... | collective-permute-start | bytes 1179656 | tf_op jit(solution)/shard_map/kv_PT_X1/ppermute | solution.py:23
  16.6 0.1 stack.37
  16.7 0.1 stack.34
  16.8 0.7 collective-permute-start.2
  17.5 6.2 %collective-permute-done.3.refs_7_ = bf16[2,128,768]{2,1,0:T(8,128)(2,1)S(1)} collective-permute-done((bf16[2,128,768]{2,1,0:T(8,128)(2,1)S(1)}, bf16[2,128,768]{2,1,0:T(8,128)(2,1)S(1)}, u32[]{:S(2)}, u32[]{:S(2)}) %collective-permute-start.3) | collective-permute-done | bytes 393248 | tf_op jit(solution)/shard_map/kv_near/ppermute | solution.py:23
  23.7 1.2 %collective-permute-start.12 = (bf16[2,128,768]{2,1,0:T(8,128)(2,1)}, bf16[2,128,768]{2,1,0:T(8,128)(2,1)S(1)}, u32[]{:S(2)}, u32[]{:S(2)}) collective-permute-start(bf16[2,128,768]{2,1,0:T(8,128)(2,1)} %copy-done.5), channel_id=1, source_target_pairs={{0,16},{8,24},{16,0},{24,8},{1,17},{9,25},{17,1},{25,9},{2,18},{10... | collective-permute-start | bytes 1179656 | tf_op jit(solution)/shard_map/qd_PT/ppermute | solution.py:27
  24.9 0.8 %collective-permute-start.9 = (bf16[2,128,768]{2,1,0:T(8,128)(2,1)S(1)}, bf16[2,128,768]{2,1,0:T(8,128)(2,1)S(1)}, u32[]{:S(2)}, u32[]{:S(2)}) collective-permute-start(bf16[2,128,768]{2,1,0:T(8,128)(2,1)S(1)} %collective-permute-done.3.refs_7_), channel_id=1, source_target_pairs={{0,8},{8,0},{16,24},{24,16},{1,9},{9,1},{17,25},{25,17},{2,10},{10... | collective-permute-start | bytes 1179656 | tf_op jit(solution)/shard_map/kvnear_X1/ppermute | solution.py:23
  25.8 2.3 %collective-permute-start.15 = (bf16[2,128,768]{2,1,0:T(8,128)(2,1)}, bf16[2,128,768]{2,1,0:T(8,128)(2,1)S(1)}, u32[]{:S(2)}, u32[]{:S(2)}) collective-permute-start(bf16[2,128,768]{2,1,0:T(8,128)(2,1)} %copy-done.5), channel_id=1, source_target_pairs={{0,1},{1,0},{2,3},{3,2},{4,5},{5,4},{6,7},{7,6},{8,9},{9,8},{10,11... | collective-permute-start | bytes 1179656 | tf_op jit(solution)/shard_map/qd_near/ppermute | solution.py:23
  28.0 3.2 %collective-permute-start.11 = (bf16[2,128,768]{2,1,0:T(8,128)(2,1)S(1)}, bf16[2,128,768]{2,1,0:T(8,128)(2,1)S(1)}, u32[]{:S(2)}, u32[]{:S(2)}) collective-permute-start(bf16[2,128,768]{2,1,0:T(8,128)(2,1)S(1)} %collective-permute-done.3.refs_7_), channel_id=1, source_target_pairs={{8,16},{16,8},{9,17},{17,9},{10,18},{18,10},{11,19},{19,11},{12,20... | collective-permute-start | bytes 1179656 | tf_op jit(solution)/shard_map/kvnear_X2/ppermute | solution.py:23
  31.3 2.8 %collective-permute-done.12.refs_2_ = bf16[2,128,768]{2,1,0:T(8,128)(2,1)S(1)} collective-permute-done((bf16[2,128,768]{2,1,0:T(8,128)(2,1)}, bf16[2,128,768]{2,1,0:T(8,128)(2,1)S(1)}, u32[]{:S(2)}, u32[]{:S(2)}) %collective-permute-start.12) | collective-permute-done | bytes 393248 | tf_op jit(solution)/shard_map/qd_PT/ppermute | solution.py:27
  34.1 1.4 %collective-permute-start.13 = (bf16[2,128,768]{2,1,0:T(8,128)(2,1)S(1)}, bf16[2,128,768]{2,1,0:T(8,128)(2,1)S(1)}, u32[]{:S(2)}, u32[]{:S(2)}) collective-permute-start(bf16[2,128,768]{2,1,0:T(8,128)(2,1)S(1)} %collective-permute-done.12.refs_2_), channel_id=1, source_target_pairs={{0,8},{8,0},{16,24},{24,16},{1,9},{9,1},{17,25},{25,17},{2,10},{10... | collective-permute-start | bytes 1179656 | tf_op jit(solution)/shard_map/qd_PT_X1/ppermute | solution.py:23
  35.6 0.2 select_reduce_fusion
  35.8 4.3 %collective-permute-start.14 = (bf16[2,128,768]{2,1,0:T(8,128)(2,1)S(1)}, bf16[2,128,768]{2,1,0:T(8,128)(2,1)S(1)}, u32[]{:S(2)}, u32[]{:S(2)}) collective-permute-start(bf16[2,128,768]{2,1,0:T(8,128)(2,1)S(1)} %collective-permute-done.2.refs_3_), channel_id=1, source_target_pairs={{8,16},{16,8},{9,17},{17,9},{10,18},{18,10},{11,19},{19,11},{12,20... | collective-permute-start | bytes 1179656 | tf_op jit(solution)/shard_map/qdfar_X2/ppermute | solution.py:23
  40.1 4.4 %shard_map.67 = (bf16[128,768]{1,0:T(8,128)(2,1)}, f32[128,128]{1,0:T(8,128)S(1)}, f32[32,128]{1,0:T(8,128)S(1)}) custom-call(f32[10]{0:T(128)S(1)} %or_select_fusion.bias_ref, bf16[128,768]{1,0:T(8,128)(2,1)S(1)} %bitcast.23, bf16[128,768]{1,0:T(8,128)(2,1)S(1)} %bitcast.27, f32[8,128]{1,0:T(8,128)S(1)} %broadcast_in_dim.57.flags_ref, ...), custom_call_target="tpu_custom_call" | custom-call | flops 128 | bytes 128 | tf_op jit(solution)/shard_map/pallas_call | solution.py:276
  44.5 4.1 %all-gather = f32[128,128]{1,0:T(8,128)S(1)} all-gather(f32[32,128]{1,0:T(8,128)S(1)} %get-tuple-element.30), channel_id=2, replica_groups=mesh['gx'=4,'gy'=8] {'gx'}, dimensions={0}, use_global_device_ids=true | all-gather | bytes 81920 | tf_op jit(solution)/shard_map/stats_row/all_gather | solution.py:295
  48.6 0.3 collective-permute-start.16
  48.9 3.6 %collective-permute-start.17 = (bf16[2,128,768]{2,1,0:T(8,128)(2,1)S(1)}, bf16[2,128,768]{2,1,0:T(8,128)(2,1)S(1)}, u32[]{:S(2)}, u32[]{:S(2)}) collective-permute-start(bf16[2,128,768]{2,1,0:T(8,128)(2,1)S(1)} %collective-permute-done.15.refs_6_), channel_id=1, source_target_pairs={{8,16},{16,8},{9,17},{17,9},{10,18},{18,10},{11,19},{19,11},{12,20... | collective-permute-start | bytes 1179656 | tf_op jit(solution)/shard_map/qdnear_X2/ppermute | solution.py:23
  52.7 0.8 %collective-permute-start.18 = (f32[4,32,128]{2,1,0:T(8,128)S(1)}, f32[4,32,128]{2,1,0:T(8,128)S(1)}, u32[]{:S(2)}, u32[]{:S(2)}) collective-permute-start(f32[4,32,128]{2,1,0:T(8,128)S(1)} %bitcast.30), channel_id=1, source_target_pairs={{1,2},{2,1},{3,4},{4,3},{5,6},{6,5},{9,10},{10,9},{11,12},{12,11},... | collective-permute-start | bytes 196616 | tf_op jit(solution)/shard_map/stats_far/ppermute | solution.py:23
  53.5 4.7 %collective-permute-start.19 = (f32[4,32,128]{2,1,0:T(8,128)S(1)}, f32[4,32,128]{2,1,0:T(8,128)S(1)}, u32[]{:S(2)}, u32[]{:S(2)}) collective-permute-start(f32[4,32,128]{2,1,0:T(8,128)S(1)} %bitcast.31), channel_id=1, source_target_pairs={{0,1},{1,0},{2,3},{3,2},{4,5},{5,4},{6,7},{7,6},{8,9},{9,8},{10,11... | collective-permute-start | bytes 196616 | tf_op jit(solution)/shard_map/stats_near/ppermute | solution.py:23
  58.3 4.7 %shard_map.68 = bf16[128,768]{1,0:T(8,128)(2,1)} custom-call(f32[10]{0:T(128)S(1)} %or_select_fusion.bias_ref, bf16[128,768]{1,0:T(8,128)(2,1)S(1)} %bitcast.24, bf16[128,768]{1,0:T(8,128)(2,1)S(1)} %bitcast.28, f32[128,128]{1,0:T(8,128)S(1)} %get-tuple-element.31.columns_ref, bf16[2,128,768]{2,1,0:T(8,128)(2,1)S(1)} %bitcast.20, ...), custom_call_target="tpu_custom_call" | custom-call | flops 128 | bytes 128 | tf_op jit(solution)/shard_map/pallas_call | solution.py:276
  63.0 5.7 %shard_map.69 = bf16[2,128,768]{2,1,0:T(8,128)(2,1)} custom-call(s32[10]{0:T(128)S(1)} %broadcast_clamp_fusion.index_ref, f32[10,128]{1,0:T(8,128)S(1)} %fusion.choose_ref, bf16[2,128,768]{2,1,0:T(8,128)(2,1)S(1)} %bitcast.21, bf16[128,768]{1,0:T(8,128)(2,1)S(1)} %bitcast.25, bf16[128,768]{1,0:T(8,128)(2,1)S(1)} %bitcast.29, ...), custom_call_target="tpu_custom_call" | custom-call | flops 128 | bytes 128 | tf_op jit(solution)/shard_map/pallas_call | solution.py:308
  (39 shorter events, 0.2 us)
Async XLA Ops:
  0.6 2.0 %collective-permute-start = (bf16[2,128,768]{2,1,0:T(8,128)(2,1)}, bf16[2,128,768]{2,1,0:T(8,128)(2,1)S(1)}, u32[]{:S(2)}, u32[]{:S(2)}) collective-permute-start(bf16[2,128,768]{2,1,0:T(8,128)(2,1)} %bitcast.15), channel_id=1, source_target_pairs={{0,8},{8,0},{16,24},{24,16},{1,9},{9,1},{17,25},{25,17},{2,10},{10... | collective-permute-start | bytes 1179656 | tf_op jit(solution)/shard_map/kv_X1/ppermute | solution.py:23
  0.8 8.6 %collective-permute-start.1 = (bf16[2,128,768]{2,1,0:T(8,128)(2,1)}, bf16[2,128,768]{2,1,0:T(8,128)(2,1)S(1)}, u32[]{:S(2)}, u32[]{:S(2)}) collective-permute-start(bf16[2,128,768]{2,1,0:T(8,128)(2,1)} %bitcast.16), channel_id=1, source_target_pairs={{1,2},{2,1},{3,4},{4,3},{5,6},{6,5},{9,10},{10,9},{11,12},{12,11},... | collective-permute-start | bytes 1179656 | tf_op jit(solution)/shard_map/kv_far/ppermute | solution.py:23
  2.6 1.4 %copy-start = (bf16[1,1,2,128,768]{4,3,2,1,0:T(8,128)(2,1)S(1)}, bf16[1,1,2,128,768]{4,3,2,1,0:T(8,128)(2,1)}, u32[]{:S(2)}) copy-start(bf16[1,1,2,128,768]{4,3,2,1,0:T(8,128)(2,1)} %param.5) | copy-start | bytes 1179652
  2.6 37.5 %copy-start.1 = (bf16[1,1,128,768]{3,2,1,0:T(8,128)(2,1)S(1)}, bf16[1,1,128,768]{3,2,1,0:T(8,128)(2,1)}, u32[]{:S(2)}) copy-start(bf16[1,1,128,768]{3,2,1,0:T(8,128)(2,1)} %param.4) | copy-start | bytes 589828
  2.6 37.5 %copy-start.2 = (bf16[1,1,128,768]{3,2,1,0:T(8,128)(2,1)S(1)}, bf16[1,1,128,768]{3,2,1,0:T(8,128)(2,1)}, u32[]{:S(2)}) copy-start(bf16[1,1,128,768]{3,2,1,0:T(8,128)(2,1)} %param.6) | copy-start | bytes 589828
  3.8 12.2 %copy-start.5 = (bf16[2,128,768]{2,1,0:T(8,128)(2,1)}, bf16[2,128,768]{2,1,0:T(8,128)(2,1)S(1)}, u32[]{:S(2)}) copy-start(bf16[2,128,768]{2,1,0:T(8,128)(2,1)S(1)} %pad_maximum_fusion) | copy-start | bytes 1179652
  3.8 5.6 %collective-permute-start.4 = (bf16[2,128,768]{2,1,0:T(8,128)(2,1)S(1)}, bf16[2,128,768]{2,1,0:T(8,128)(2,1)S(1)}, u32[]{:S(2)}, u32[]{:S(2)}) collective-permute-start(bf16[2,128,768]{2,1,0:T(8,128)(2,1)S(1)} %pad_maximum_fusion), channel_id=1, source_target_pairs={{0,8},{8,0},{16,24},{24,16},{1,9},{9,1},{17,25},{25,17},{2,10},{10... | collective-permute-start | bytes 1179656 | tf_op jit(solution)/shard_map/qd_X1/ppermute | solution.py:23
  4.0 11.9 %collective-permute-start.7 = (bf16[2,128,768]{2,1,0:T(8,128)(2,1)S(1)}, bf16[2,128,768]{2,1,0:T(8,128)(2,1)S(1)}, u32[]{:S(2)}, u32[]{:S(2)}) collective-permute-start(bf16[2,128,768]{2,1,0:T(8,128)(2,1)S(1)} %bitcast.17), channel_id=1, source_target_pairs={{0,16},{8,24},{16,0},{24,8},{1,17},{9,25},{17,1},{25,9},{2,18},{10... | collective-permute-start | bytes 1179656 | tf_op jit(solution)/shard_map/kv_PT/ppermute | solution.py:27
  6.6 17.1 %collective-permute-start.3 = (bf16[2,128,768]{2,1,0:T(8,128)(2,1)S(1)}, bf16[2,128,768]{2,1,0:T(8,128)(2,1)S(1)}, u32[]{:S(2)}, u32[]{:S(2)}) collective-permute-start(bf16[2,128,768]{2,1,0:T(8,128)(2,1)S(1)} %bitcast.18), channel_id=1, source_target_pairs={{0,1},{1,0},{2,3},{3,2},{4,5},{5,4},{6,7},{7,6},{8,9},{9,8},{10,11... | collective-permute-start | bytes 1179656 | tf_op jit(solution)/shard_map/kv_near/ppermute | solution.py:23
  9.4 0.7 %copy-start.3 = (bf16[2,128,768]{2,1,0:T(8,128)(2,1)}, bf16[2,128,768]{2,1,0:T(8,128)(2,1)S(1)}, u32[]{:S(2)}) copy-start(bf16[2,128,768]{2,1,0:T(8,128)(2,1)S(1)} %collective-permute-done.4.refs_0_) | copy-start | bytes 1179652
  10.1 14.8 %collective-permute-start.5 = (bf16[2,128,768]{2,1,0:T(8,128)(2,1)S(1)}, bf16[2,128,768]{2,1,0:T(8,128)(2,1)S(1)}, u32[]{:S(2)}, u32[]{:S(2)}) collective-permute-start(bf16[2,128,768]{2,1,0:T(8,128)(2,1)S(1)} %collective-permute-done.1.refs_4_), channel_id=1, source_target_pairs={{0,8},{8,0},{16,24},{24,16},{1,9},{9,1},{17,25},{25,17},{2,10},{10... | collective-permute-start | bytes 1179656 | tf_op jit(solution)/shard_map/kvfar_X1/ppermute | solution.py:23
  10.9 14.0 %collective-permute-start.6 = (bf16[2,128,768]{2,1,0:T(8,128)(2,1)S(1)}, bf16[2,128,768]{2,1,0:T(8,128)(2,1)S(1)}, u32[]{:S(2)}, u32[]{:S(2)}) collective-permute-start(bf16[2,128,768]{2,1,0:T(8,128)(2,1)S(1)} %collective-permute-done.1.refs_4_), channel_id=1, source_target_pairs={{8,16},{16,8},{9,17},{17,9},{10,18},{18,10},{11,19},{19,11},{12,20... | collective-permute-start | bytes 1179656 | tf_op jit(solution)/shard_map/kvfar_X2/ppermute | solution.py:23
  15.9 9.0 %collective-permute-start.8 = (bf16[2,128,768]{2,1,0:T(8,128)(2,1)S(1)}, bf16[2,128,768]{2,1,0:T(8,128)(2,1)S(1)}, u32[]{:S(2)}, u32[]{:S(2)}) collective-permute-start(bf16[2,128,768]{2,1,0:T(8,128)(2,1)S(1)} %collective-permute-done.7.refs_3_), channel_id=1, source_target_pairs={{0,8},{8,0},{16,24},{24,16},{1,9},{9,1},{17,25},{25,17},{2,10},{10... | collective-permute-start | bytes 1179656 | tf_op jit(solution)/shard_map/kv_PT_X1/ppermute | solution.py:23
  16.7 9.0 %copy-start.6 = (s32[1,1,9]{2,1,0:T(1,128)S(1)}, s32[1,1,9]{2,1,0:T(1,128)}, u32[]{:S(2)}) copy-start(s32[1,1,9]{2,1,0:T(1,128)} %param.7) | copy-start | bytes 112
  16.8 18.7 %collective-permute-start.2 = (bf16[2,128,768]{2,1,0:T(8,128)(2,1)}, bf16[2,128,768]{2,1,0:T(8,128)(2,1)S(1)}, u32[]{:S(2)}, u32[]{:S(2)}) collective-permute-start(bf16[2,128,768]{2,1,0:T(8,128)(2,1)} %copy-done.5), channel_id=1, source_target_pairs={{1,2},{2,1},{3,4},{4,3},{5,6},{6,5},{9,10},{10,9},{11,12},{12,11},... | collective-permute-start | bytes 1179656 | tf_op jit(solution)/shard_map/qd_far/ppermute | solution.py:23
  23.7 10.4 %collective-permute-start.12 = (bf16[2,128,768]{2,1,0:T(8,128)(2,1)}, bf16[2,128,768]{2,1,0:T(8,128)(2,1)S(1)}, u32[]{:S(2)}, u32[]{:S(2)}) collective-permute-start(bf16[2,128,768]{2,1,0:T(8,128)(2,1)} %copy-done.5), channel_id=1, source_target_pairs={{0,16},{8,24},{16,0},{24,8},{1,17},{9,25},{17,1},{25,9},{2,18},{10... | collective-permute-start | bytes 1179656 | tf_op jit(solution)/shard_map/qd_PT/ppermute | solution.py:27
  24.9 10.6 %collective-permute-start.9 = (bf16[2,128,768]{2,1,0:T(8,128)(2,1)S(1)}, bf16[2,128,768]{2,1,0:T(8,128)(2,1)S(1)}, u32[]{:S(2)}, u32[]{:S(2)}) collective-permute-start(bf16[2,128,768]{2,1,0:T(8,128)(2,1)S(1)} %collective-permute-done.3.refs_7_), channel_id=1, source_target_pairs={{0,8},{8,0},{16,24},{24,16},{1,9},{9,1},{17,25},{25,17},{2,10},{10... | collective-permute-start | bytes 1179656 | tf_op jit(solution)/shard_map/kvnear_X1/ppermute | solution.py:23
  25.8 22.8 %collective-permute-start.15 = (bf16[2,128,768]{2,1,0:T(8,128)(2,1)}, bf16[2,128,768]{2,1,0:T(8,128)(2,1)S(1)}, u32[]{:S(2)}, u32[]{:S(2)}) collective-permute-start(bf16[2,128,768]{2,1,0:T(8,128)(2,1)} %copy-done.5), channel_id=1, source_target_pairs={{0,1},{1,0},{2,3},{3,2},{4,5},{5,4},{6,7},{7,6},{8,9},{9,8},{10,11... | collective-permute-start | bytes 1179656 | tf_op jit(solution)/shard_map/qd_near/ppermute | solution.py:23
  28.0 12.1 %collective-permute-start.11 = (bf16[2,128,768]{2,1,0:T(8,128)(2,1)S(1)}, bf16[2,128,768]{2,1,0:T(8,128)(2,1)S(1)}, u32[]{:S(2)}, u32[]{:S(2)}) collective-permute-start(bf16[2,128,768]{2,1,0:T(8,128)(2,1)S(1)} %collective-permute-done.3.refs_7_), channel_id=1, source_target_pairs={{8,16},{16,8},{9,17},{17,9},{10,18},{18,10},{11,19},{19,11},{12,20... | collective-permute-start | bytes 1179656 | tf_op jit(solution)/shard_map/kvnear_X2/ppermute | solution.py:23
  34.1 10.4 %collective-permute-start.13 = (bf16[2,128,768]{2,1,0:T(8,128)(2,1)S(1)}, bf16[2,128,768]{2,1,0:T(8,128)(2,1)S(1)}, u32[]{:S(2)}, u32[]{:S(2)}) collective-permute-start(bf16[2,128,768]{2,1,0:T(8,128)(2,1)S(1)} %collective-permute-done.12.refs_2_), channel_id=1, source_target_pairs={{0,8},{8,0},{16,24},{24,16},{1,9},{9,1},{17,25},{25,17},{2,10},{10... | collective-permute-start | bytes 1179656 | tf_op jit(solution)/shard_map/qd_PT_X1/ppermute | solution.py:23
  35.5 4.6 %collective-permute-start.10 = (bf16[2,128,768]{2,1,0:T(8,128)(2,1)S(1)}, bf16[2,128,768]{2,1,0:T(8,128)(2,1)S(1)}, u32[]{:S(2)}, u32[]{:S(2)}) collective-permute-start(bf16[2,128,768]{2,1,0:T(8,128)(2,1)S(1)} %collective-permute-done.2.refs_3_), channel_id=1, source_target_pairs={{0,8},{8,0},{16,24},{24,16},{1,9},{9,1},{17,25},{25,17},{2,10},{10... | collective-permute-start | bytes 1179656 | tf_op jit(solution)/shard_map/qdfar_X1/ppermute | solution.py:23
  35.8 27.2 %collective-permute-start.14 = (bf16[2,128,768]{2,1,0:T(8,128)(2,1)S(1)}, bf16[2,128,768]{2,1,0:T(8,128)(2,1)S(1)}, u32[]{:S(2)}, u32[]{:S(2)}) collective-permute-start(bf16[2,128,768]{2,1,0:T(8,128)(2,1)S(1)} %collective-permute-done.2.refs_3_), channel_id=1, source_target_pairs={{8,16},{16,8},{9,17},{17,9},{10,18},{18,10},{11,19},{19,11},{12,20... | collective-permute-start | bytes 1179656 | tf_op jit(solution)/shard_map/qdfar_X2/ppermute | solution.py:23
  48.6 14.4 %collective-permute-start.16 = (bf16[2,128,768]{2,1,0:T(8,128)(2,1)S(1)}, bf16[2,128,768]{2,1,0:T(8,128)(2,1)S(1)}, u32[]{:S(2)}, u32[]{:S(2)}) collective-permute-start(bf16[2,128,768]{2,1,0:T(8,128)(2,1)S(1)} %collective-permute-done.15.refs_6_), channel_id=1, source_target_pairs={{0,8},{8,0},{16,24},{24,16},{1,9},{9,1},{17,25},{25,17},{2,10},{10... | collective-permute-start | bytes 1179656 | tf_op jit(solution)/shard_map/qdnear_X1/ppermute | solution.py:23
  48.9 14.0 %collective-permute-start.17 = (bf16[2,128,768]{2,1,0:T(8,128)(2,1)S(1)}, bf16[2,128,768]{2,1,0:T(8,128)(2,1)S(1)}, u32[]{:S(2)}, u32[]{:S(2)}) collective-permute-start(bf16[2,128,768]{2,1,0:T(8,128)(2,1)S(1)} %collective-permute-done.15.refs_6_), channel_id=1, source_target_pairs={{8,16},{16,8},{9,17},{17,9},{10,18},{18,10},{11,19},{19,11},{12,20... | collective-permute-start | bytes 1179656 | tf_op jit(solution)/shard_map/qdnear_X2/ppermute | solution.py:23
  52.7 10.3 %collective-permute-start.18 = (f32[4,32,128]{2,1,0:T(8,128)S(1)}, f32[4,32,128]{2,1,0:T(8,128)S(1)}, u32[]{:S(2)}, u32[]{:S(2)}) collective-permute-start(f32[4,32,128]{2,1,0:T(8,128)S(1)} %bitcast.30), channel_id=1, source_target_pairs={{1,2},{2,1},{3,4},{4,3},{5,6},{6,5},{9,10},{10,9},{11,12},{12,11},... | collective-permute-start | bytes 196616 | tf_op jit(solution)/shard_map/stats_far/ppermute | solution.py:23
  53.5 9.5 %collective-permute-start.19 = (f32[4,32,128]{2,1,0:T(8,128)S(1)}, f32[4,32,128]{2,1,0:T(8,128)S(1)}, u32[]{:S(2)}, u32[]{:S(2)}) collective-permute-start(f32[4,32,128]{2,1,0:T(8,128)S(1)} %bitcast.31), channel_id=1, source_target_pairs={{0,1},{1,0},{2,3},{3,2},{4,5},{5,4},{6,7},{7,6},{8,9},{9,8},{10,11... | collective-permute-start | bytes 196616 | tf_op jit(solution)/shard_map/stats_near/ppermute | solution.py:23
  58.3 4.7 %copy-start.4 = (bf16[2,128,768]{2,1,0:T(8,128)(2,1)S(1)}, bf16[2,128,768]{2,1,0:T(8,128)(2,1)}, u32[]{:S(2)}) copy-start(bf16[2,128,768]{2,1,0:T(8,128)(2,1)} %copy-done.3) | copy-start | bytes 1179652
